TPU v7x, 512 devices: a whole 4x4x16 slice. The times are simulated.
512 devices in a mesh: tok: 16 (over z_hi, y), feat: 32 (over x, z_lo, core).
Axes of the slice: x: 4, y: 4, z: 16 (z_hi: 4, z_lo: 4; z = z_hi * 4 + z_lo), core: 2. Of those that a mesh axis runs over, the one named last changes fastest.
Arguments:
- tokens: bfloat16 [1024, 8192], P('tok', 'feat'), may hold values from -6 to 6
- gain: float32 [8192], replicated, may hold values from 0.1 to 1.9
- proj: bfloat16 [8192, 8192], P('tok', 'feat'), may hold values from -0.0625 to 0.0625
- panel_index: int32 [1], replicated, may hold values from 0 to 31
Outputs:
- panel_rows: float32 [256, 8192], P(None, 'feat')
- solved_cross: float32 [256, 8192], P(None, 'feat')
All inputs are finite; a program needn't handle non-finite values.
Results may differ from a plain program's by a relative error of at most 0.01.
Values may be sent and summed in bfloat16 or wider, within the bound.
No kernel may reach another device: no remote copies, remote signals or barrier semaphores. Data moves between devices by JAX's collectives and lax.ppermute only.
A program may use at most 64 MiB of HBM per device.

v0:
```python
import math

import jax
import jax.numpy as jnp
import numpy as np
from jax import lax
from jax.experimental import pallas as pl
from jax.experimental.pallas import tpu as pltpu
from jax.sharding import Mesh
from jax.sharding import PartitionSpec as P

D = 8192
PANEL = 256
TOKENS = 1024
AXES = ("zh", "y", "x", "zl", "c")
TOK = ("zh", "y")
FEAT = ("x", "zl", "c")
NB = 64
STEP = 8
F32 = jnp.float32
BF16 = jnp.bfloat16
HIGHEST = lax.Precision.HIGHEST


def swap(value, axis, bits, size=4):
    return lax.ppermute(value, axis, [(i, i ^ bits) for i in range(size)])


def double(value, axis, bits):
    return jnp.concatenate([value, swap(value, axis, bits)], axis=0)


def merge(mine, other):
    return jnp.concatenate([mine[:64] + other[:64], mine[64:], other[64:]], axis=0)


def call(kernel, outs, *args, n_scalars=0, scratch=(), final=False):
    vmem = pl.BlockSpec(memory_space=pltpu.VMEM)
    smem = pl.BlockSpec(memory_space=pltpu.SMEM)
    many = isinstance(outs, tuple)
    args = args[:n_scalars] + tuple(
        pltpu.with_memory_space_constraint(a, pltpu.VMEM) for a in args[n_scalars:]
    )
    if not final:
        kept = [pltpu.VMEM(o.shape, o.dtype) for o in (outs if many else (outs,))]
        outs = tuple(kept) if many else kept[0]
    return pl.pallas_call(
        kernel,
        out_shape=outs,
        in_specs=[smem] * n_scalars + [vmem] * (len(args) - n_scalars),
        out_specs=tuple(vmem for _ in outs) if many else vmem,
        scratch_shapes=list(scratch),
    )(*args)


def dot_tn(a, b):
    return lax.dot_general(a, b, (((0,), (0,)), ((), ())), preferred_element_type=F32)


def project_kernel(mine, other, gain, p0, p1, far, keep, s1, s2, s3, acc, sq):
    zh, y, x, zl, c = [lax.axis_index(a) for a in AXES]
    total = jnp.zeros((256, 256), F32)
    squares = jnp.zeros((256, 256), F32)
    for y_rel, (proj, at) in enumerate(((p0, 0), (p1, 0), (far, 512), (far, 0))):
        zl_there = y ^ y_rel
        z_rel = zl ^ zl_there
        for c_rel, src in enumerate((mine, other)):
            c_there = c ^ c_rel
            rows = [
                src[pl.ds(pl.multiple_of(64 + (at_x * 4 + z_rel) * 64, 64), 64), :]
                for at_x in (0, 1, 3, 2)
            ]
            raw = jnp.concatenate(rows, axis=0).astype(F32)
            squares = squares + raw * raw
            scale = gain[pl.ds(8 * zh + 2 * zl_there + c_there, 1), :]
            scaled = (raw * scale).astype(BF16)
            weights = proj[pl.ds(pl.multiple_of(at + c_there * 256, 256), 256), :]
            total = total + jnp.dot(scaled, weights, preferred_element_type=F32)
    acc[...] = total
    sq[...] = jnp.broadcast_to(jnp.sum(squares, axis=1, keepdims=True), (256, 256))
    row = lax.broadcasted_iota(jnp.int32, (64, 256), 0)
    lane = lax.broadcasted_iota(jnp.int32, (64, 256), 1)
    for step, out in enumerate((keep, s1, s2, s3)):
        at = pl.multiple_of((x ^ zh ^ step) * 64, 64)
        part = acc[pl.ds(at, 64), :]
        norm = sq[pl.ds(at, 64), :]
        high = norm.astype(BF16).astype(F32)
        spread = jnp.where(lane == row, high, jnp.where(lane == row + 64, norm - high, 0.0))
        line = jnp.sum(spread, axis=0, keepdims=True)
        out[0:64, :] = part.astype(out.dtype)
        out[64:80, :] = jnp.broadcast_to(line, (16, 256)).astype(out.dtype)
        if step:
            out[80:144, :] = mine[0:64, :] + other[0:64, :]


def change_kernel(tokens, keep, r1, r2, r3, change):
    total = keep[...]
    for part in (r1, r2, r3):
        total = total + part[0:80, :].astype(F32)
    row = lax.broadcasted_iota(jnp.int32, (64, 256), 0)
    lane = lax.broadcasted_iota(jnp.int32, (64, 256), 1)
    line = jnp.broadcast_to(total[64:65, :], (64, 256))
    picked = jnp.where((lane == row) | (lane == row + 64), line, 0.0)
    square_sum = jnp.sum(picked, axis=1, keepdims=True)
    inv_rms = lax.rsqrt(square_sum / D + 1e-05)
    own = tokens[...].astype(F32)
    outputs = (own + total[0:64, :] * inv_rms).astype(BF16)
    change[...] = (outputs.astype(F32) - own).astype(BF16)


def invert_block(block):
    row = lax.broadcasted_iota(jnp.int32, (NB, 2 * NB), 0)
    lane = lax.broadcasted_iota(jnp.int32, (NB, 2 * NB), 1)
    eye = jnp.where(lane[:, :NB] == row[:, :NB], 1.0, 0.0).astype(F32)
    work = jnp.concatenate([block, eye], axis=1)
    for j in range(0, NB, STEP):
        columns = [jnp.broadcast_to(work[:, k : k + 1], work.shape) for k in range(j, j + STEP)]
        pivots = [work[k : k + 1, :] for k in range(j, j + STEP)]
        for i in range(STEP):
            scale = lax.rsqrt(columns[i][j + i : j + i + 1, :])
            pivots[i] = pivots[i] * scale
            columns[i] = columns[i] * scale
            for k in range(i + 1, STEP):
                factor = columns[i][j + k : j + k + 1, :]
                pivots[k] = pivots[k] - factor * pivots[i]
                columns[k] = columns[k] - factor * columns[i]
        update = columns[0] * pivots[0]
        for i in range(1, STEP):
            update = update + columns[i] * pivots[i]
        after = jnp.where(row >= j + STEP, work - update, work)
        for i in range(STEP):
            after = jnp.where(row == j + i, pivots[i], after)
        work = after
    return work[:, NB:]


def dot_hi(a, b, dims=((1,), (0,))):
    return lax.dot_general(a, b, (dims, ((), ())), precision=HIGHEST, preferred_element_type=F32)


def factor_kernel(b0, b1, inverse, schur):
    total = dot_tn(b0[...], b0[...]) + dot_tn(b1[...], b1[...])
    row = lax.broadcasted_iota(jnp.int32, (PANEL, PANEL), 0)
    lane = lax.broadcasted_iota(jnp.int32, (PANEL, PANEL), 1)
    schur[...] = total / TOKENS + jnp.where(row == lane, 0.1, 0.0)
    inverse[...] = jnp.where(row == lane, 1.0, 0.0)
    for k in range(PANEL // NB):
        lo, hi = k * NB, (k + 1) * NB
        block_inverse = invert_block(schur[lo:hi, lo:hi])
        top = dot_hi(block_inverse, inverse[lo:hi, :])
        inverse[lo:hi, :] = top
        if hi < PANEL:
            below = dot_hi(schur[hi:, lo:hi], block_inverse, ((1,), (1,)))
            schur[hi:, hi:] = schur[hi:, hi:] - dot_hi(below, below, ((1,), (1,)))
            inverse[hi:, :] = inverse[hi:, :] - dot_hi(below, top)


def gram_kernel(is_band, b0, b1, t0, t1, inverse, out):
    total = dot_tn(b0[...], t0[...]) + dot_tn(b1[...], t1[...])
    row = lax.broadcasted_iota(jnp.int32, (PANEL, PANEL), 0)
    lane = lax.broadcasted_iota(jnp.int32, (PANEL, PANEL), 1)
    ridge = jnp.where((row == lane) & (is_band[0] == 1), 0.1, 0.0)
    out[...] = dot_hi(inverse[...], total / TOKENS + ridge)


def cross_kernel(b0, b1, c0, c1, c2, c3, inverse, out):
    total = dot_tn(b0[0:256, :], c0[...]) + dot_tn(b0[256:512, :], c1[...])
    total = total + dot_tn(b1[0:256, :], c2[...]) + dot_tn(b1[256:512, :], c3[...])
    out[...] = dot_hi(inverse[...], total * (math.sqrt(D) / TOKENS))


def steps(tokens, gain, proj, panel_index):
    _, _, x, zl, c = [lax.axis_index(a).astype(jnp.int32) for a in AXES]
    is_band = panel_index[0].astype(jnp.int32) == 8 * x + 2 * zl + c
    band = jnp.where(is_band, tokens, jnp.zeros_like(tokens))
    gains = gain.reshape(32, 256)

    turned = lax.ppermute(
        tokens,
        AXES,
        [
            ((((a * 4 + b) * 4 + d) * 8 + e), (((d * 4 + b) * 4 + a) * 8 + e))
            for a in range(4)
            for b in range(4)
            for d in range(4)
            for e in range(8)
        ],
    )
    weights = [proj, swap(proj, "y", 1)]

    load = jnp.concatenate([band, turned], axis=0)
    load, gains = lax.optimization_barrier((load, gains))
    load = merge(load, swap(load, "zl", 1))
    load, weights = lax.optimization_barrier((load, weights))
    weights.append(swap(jnp.concatenate(weights, axis=0), "y", 3))
    load = merge(load, swap(load, "zl", 2))
    there = swap(load, "x", 1)
    blocks = double(tokens, "zh", 1)
    load, blocks = lax.optimization_barrier((merge(load, there), blocks))
    there = swap(load, "x", 3)
    blocks = double(blocks, "zh", 3)
    load = merge(load, there)
    band = load[:64]
    other = swap(load, "c", 1, 2)
    band = band + other[:64]

    part = jax.ShapeDtypeStruct((144, 256), BF16)
    keep, s1, s2, s3 = call(
        project_kernel,
        (jax.ShapeDtypeStruct((80, 256), F32), part, part, part),
        load,
        other,
        gains,
        *weights,
        scratch=(pltpu.VMEM((256, 256), F32), pltpu.VMEM((256, 256), F32)),
    )
    r2, r1, r3 = swap(s2, "zh", 2), swap(s1, "zh", 1), swap(s3, "zh", 3)
    blocks = double(blocks, "y", 1)
    blocks = [blocks, swap(blocks, "y", 3)]
    bands = jnp.concatenate([band] + [r[80:144] for r in (r1, r3, r2)], axis=0)
    bands = double(bands, "y", 1)
    bands = [bands, swap(bands, "y", 3)]

    change = call(change_kernel, jax.ShapeDtypeStruct((64, 256), BF16), tokens, keep, r1, r2, r3)
    change = double(change, "zh", 1)
    change = double(change, "zh", 3)
    changes = [change] + [swap(change, "y", k) for k in (1, 3, 2)]

    square = jax.ShapeDtypeStruct((PANEL, PANEL), F32)
    inverse = call(factor_kernel, square, *bands, scratch=(pltpu.VMEM((PANEL, PANEL), F32),))
    flag = is_band.astype(jnp.int32).reshape(1)
    panel_rows = call(gram_kernel, square, flag, *bands, *blocks, inverse, n_scalars=1, final=True)
    solved_cross = call(cross_kernel, square, *bands, *changes, inverse, final=True)
    return (panel_rows, solved_cross)


def solution(mesh):
    split = Mesh(np.asarray(mesh.devices).reshape(4, 4, 4, 4, 2), AXES)
    return jax.shard_map(
        steps,
        mesh=split,
        in_specs=(P(TOK, FEAT), P(), P(TOK, FEAT), P()),
        out_specs=(P(None, FEAT), P(None, FEAT)),
        check_vma=False,
    )
```

profile of v0, /device:TPU:6, one launch (start us, length us, event | category | flops | bytes accessed | tf_op | source)
XLA Modules:
  0.0 160.4 jit_solution(8894471621238781891)
XLA Ops:
  0.6 12.7 %collective-permute-start = (bf16[64,256]{1,0:T(8,128)(2,1)}, bf16[64,256]{1,0:T(8,128)(2,1)S(1)}, u32[]{:S(2)}, u32[]{:S(2)}) collective-permute-start(bf16[64,256]{1,0:T(8,128)(2,1)} %tokens.1), channel_id=1, source_target_pairs={{0,0},{1,1},{2,2},{3,3},{4,4},{5,5},{6,6},{7,7},{8,128},{9,129},{1... | collective-permute-start | bytes 98312 | tf_op jit(solution)/shard_map/ppermute | solution.py:178
  14.0 0.8 reshape.14.gain
  14.7 1.5 collective-permute-done
  16.2 2.2 %collective-permute-start.1 = (bf16[128,256]{1,0:T(8,128)(2,1)S(1)}, bf16[128,256]{1,0:T(8,128)(2,1)S(1)}, u32[]{:S(2)}, u32[]{:S(2)}) collective-permute-start(bf16[128,256]{1,0:T(8,128)(2,1)S(1)} %pad_maximum_fusion.8), channel_id=1, source_target_pairs={{0,2},{2,0},{4,6},{6,4},{1,3},{3,1},{5,7},{7,5},{8,10},{10,8},{12,... | collective-permute-start | bytes 196616 | tf_op jit(solution)/shard_map/ppermute | solution.py:26
  18.4 3.5 %collective-permute-start.2 = (bf16[512,256]{1,0:T(8,128)(2,1)}, bf16[512,256]{1,0:T(8,128)(2,1)S(1)}, u32[]{:S(2)}, u32[]{:S(2)}) collective-permute-start(bf16[512,256]{1,0:T(8,128)(2,1)} %p0), channel_id=1, source_target_pairs={{0,32},{32,0},{64,96},{96,64},{1,33},{33,1},{65,97},{97,65},{2,34}... | collective-permute-start | bytes 786440 | tf_op jit(solution)/shard_map/ppermute | solution.py:26
  21.9 1.4 collective-permute-done.1
  23.3 4.1 %collective-permute-done.2.p1 = bf16[512,256]{1,0:T(8,128)(2,1)S(1)} collective-permute-done((bf16[512,256]{1,0:T(8,128)(2,1)}, bf16[512,256]{1,0:T(8,128)(2,1)S(1)}, u32[]{:S(2)}, u32[]{:S(2)}) %collective-permute-start.2) | collective-permute-done | bytes 262176 | tf_op jit(solution)/shard_map/ppermute | solution.py:26
  27.4 4.5 %collective-permute-start.3 = (bf16[192,256]{1,0:T(8,128)(2,1)S(1)}, bf16[192,256]{1,0:T(8,128)(2,1)S(1)}, u32[]{:S(2)}, u32[]{:S(2)}) collective-permute-start(bf16[192,256]{1,0:T(8,128)(2,1)S(1)} %pad_maximum_fusion.7), channel_id=1, source_target_pairs={{0,4},{2,6},{4,0},{6,2},{1,5},{3,7},{5,1},{7,3},{8,12},{10,14},{12... | collective-permute-start | bytes 294920 | tf_op jit(solution)/shard_map/ppermute | solution.py:26
  31.9 3.9 %collective-permute-done.3 = bf16[192,256]{1,0:T(8,128)(2,1)S(1)} collective-permute-done((bf16[192,256]{1,0:T(8,128)(2,1)S(1)}, bf16[192,256]{1,0:T(8,128)(2,1)S(1)}, u32[]{:S(2)}, u32[]{:S(2)}) %collective-permute-start.3) | collective-permute-done | bytes 98336 | tf_op jit(solution)/shard_map/ppermute | solution.py:26
  35.9 6.0 %collective-permute-start.4 = (bf16[320,256]{1,0:T(8,128)(2,1)S(1)}, bf16[320,256]{1,0:T(8,128)(2,1)S(1)}, u32[]{:S(2)}, u32[]{:S(2)}) collective-permute-start(bf16[320,256]{1,0:T(8,128)(2,1)S(1)} %pad_maximum_fusion.3), channel_id=1, source_target_pairs={{0,8},{8,0},{16,24},{24,16},{1,9},{9,1},{17,25},{25,17},{2,10},{10... | collective-permute-start | bytes 491528 | tf_op jit(solution)/shard_map/ppermute | solution.py:26
  41.9 8.3 %collective-permute-start.5 = (bf16[64,256]{1,0:T(8,128)(2,1)S(1)}, bf16[64,256]{1,0:T(8,128)(2,1)S(1)}, u32[]{:S(2)}, u32[]{:S(2)}) collective-permute-start(bf16[64,256]{1,0:T(8,128)(2,1)S(1)} %copy-done.1), channel_id=1, source_target_pairs={{0,128},{128,0},{256,384},{384,256},{1,129},{129,1},{257,385},{385... | collective-permute-start | bytes 98312 | tf_op jit(solution)/shard_map/ppermute | solution.py:26
  50.2 1.9 %collective-permute-done.5 = bf16[64,256]{1,0:T(8,128)(2,1)S(1)} collective-permute-done((bf16[64,256]{1,0:T(8,128)(2,1)S(1)}, bf16[64,256]{1,0:T(8,128)(2,1)S(1)}, u32[]{:S(2)}, u32[]{:S(2)}) %collective-permute-start.5) | collective-permute-done | bytes 32800 | tf_op jit(solution)/shard_map/ppermute | solution.py:26
  52.1 0.0 collective-permute-done.4
  52.2 1.9 %collective-permute-start.6 = (bf16[576,256]{1,0:T(8,128)(2,1)S(1)}, bf16[576,256]{1,0:T(8,128)(2,1)S(1)}, u32[]{:S(2)}, u32[]{:S(2)}) collective-permute-start(bf16[576,256]{1,0:T(8,128)(2,1)S(1)} %pad_maximum_fusion.2), channel_id=1, source_target_pairs={{0,24},{8,16},{16,8},{24,0},{1,25},{9,17},{17,9},{25,1},{2,26},{10... | collective-permute-start | bytes 884744 | tf_op jit(solution)/shard_map/ppermute | solution.py:26
  54.1 7.9 %collective-permute-done.6 = bf16[576,256]{1,0:T(8,128)(2,1)S(1)} collective-permute-done((bf16[576,256]{1,0:T(8,128)(2,1)S(1)}, bf16[576,256]{1,0:T(8,128)(2,1)S(1)}, u32[]{:S(2)}, u32[]{:S(2)}) %collective-permute-start.6) | collective-permute-done | bytes 294944 | tf_op jit(solution)/shard_map/ppermute | solution.py:26
  62.0 0.0 copy-start
  62.1 2.1 %collective-permute-start.7 = (bf16[1088,256]{1,0:T(8,128)(2,1)S(1)}, bf16[1088,256]{1,0:T(8,128)(2,1)S(1)}, u32[]{:S(2)}, u32[]{:S(2)}) collective-permute-start(bf16[1088,256]{1,0:T(8,128)(2,1)S(1)} %pad_maximum_fusion.mine), channel_id=1, source_target_pairs={{0,1},{1,0},{2,3},{3,2},{4,5},{5,4},{6,7},{7,6},{8,9},{9,8},{10,11... | collective-permute-start | bytes 1671176 | tf_op jit(solution)/shard_map/ppermute | solution.py:26
  64.2 4.9 %collective-permute-start.8 = (bf16[1024,256]{1,0:T(8,128)(2,1)S(1)}, bf16[1024,256]{1,0:T(8,128)(2,1)S(1)}, u32[]{:S(2)}, u32[]{:S(2)}) collective-permute-start(bf16[1024,256]{1,0:T(8,128)(2,1)S(1)} %pad_maximum_fusion.1), channel_id=1, source_target_pairs={{0,96},{32,64},{64,32},{96,0},{1,97},{33,65},{65,33},{97,1},{2,98}... | collective-permute-start | bytes 1572872 | tf_op jit(solution)/shard_map/ppermute | solution.py:26
  69.1 8.9 %collective-permute-start.14 = (bf16[128,256]{1,0:T(8,128)(2,1)S(1)}, bf16[128,256]{1,0:T(8,128)(2,1)S(1)}, u32[]{:S(2)}, u32[]{:S(2)}) collective-permute-start(bf16[128,256]{1,0:T(8,128)(2,1)S(1)} %pad_maximum_fusion.9), channel_id=1, source_target_pairs={{0,384},{128,256},{256,128},{384,0},{1,385},{129,257},{257,129},{3... | collective-permute-start | bytes 196616 | tf_op jit(solution)/shard_map/ppermute | solution.py:26
  78.1 5.4 %collective-permute-done.14 = bf16[128,256]{1,0:T(8,128)(2,1)S(1)} collective-permute-done((bf16[128,256]{1,0:T(8,128)(2,1)S(1)}, bf16[128,256]{1,0:T(8,128)(2,1)S(1)}, u32[]{:S(2)}, u32[]{:S(2)}) %collective-permute-start.14) | collective-permute-done | bytes 65568 | tf_op jit(solution)/shard_map/ppermute | solution.py:26
  83.6 2.0 %collective-permute-start.15 = (bf16[256,256]{1,0:T(8,128)(2,1)S(1)}, bf16[256,256]{1,0:T(8,128)(2,1)S(1)}, u32[]{:S(2)}, u32[]{:S(2)}) collective-permute-start(bf16[256,256]{1,0:T(8,128)(2,1)S(1)} %pad_maximum_fusion.5), channel_id=1, source_target_pairs={{0,32},{32,0},{64,96},{96,64},{1,33},{33,1},{65,97},{97,65},{2,34}... | collective-permute-start | bytes 393224 | tf_op jit(solution)/shard_map/ppermute | solution.py:26
  85.6 0.0 collective-permute-done.8.far
  85.6 0.0 collective-permute-done.7.other
  85.6 0.6 shard_map.59
  86.2 6.8 %collective-permute-start.11 = (bf16[144,256]{1,0:T(8,128)(2,1)S(1)}, bf16[144,256]{1,0:T(8,128)(2,1)S(1)}, u32[]{:S(2)}, u32[]{:S(2)}) collective-permute-start(bf16[144,256]{1,0:T(8,128)(2,1)S(1)} %get-tuple-element.21), channel_id=1, source_target_pairs={{0,256},{128,384},{256,0},{384,128},{1,257},{129,385},{257,1},{385... | collective-permute-start | bytes 221192 | tf_op jit(solution)/shard_map/ppermute | solution.py:26
  93.0 7.2 %collective-permute-start.10 = (bf16[144,256]{1,0:T(8,128)(2,1)S(1)}, bf16[144,256]{1,0:T(8,128)(2,1)S(1)}, u32[]{:S(2)}, u32[]{:S(2)}) collective-permute-start(bf16[144,256]{1,0:T(8,128)(2,1)S(1)} %get-tuple-element.20), channel_id=1, source_target_pairs={{0,384},{128,256},{256,128},{384,0},{1,385},{129,257},{257,129},{3... | collective-permute-start | bytes 221192 | tf_op jit(solution)/shard_map/ppermute | solution.py:26
  100.2 3.5 %collective-permute-start.9 = (bf16[144,256]{1,0:T(8,128)(2,1)S(1)}, bf16[144,256]{1,0:T(8,128)(2,1)S(1)}, u32[]{:S(2)}, u32[]{:S(2)}) collective-permute-start(bf16[144,256]{1,0:T(8,128)(2,1)S(1)} %get-tuple-element.19), channel_id=1, source_target_pairs={{0,128},{128,0},{256,384},{384,256},{1,129},{129,1},{257,385},{385... | collective-permute-start | bytes 221192 | tf_op jit(solution)/shard_map/ppermute | solution.py:26
  103.7 6.9 %collective-permute-done.9.r1 = bf16[144,256]{1,0:T(8,128)(2,1)S(1)} collective-permute-done((bf16[144,256]{1,0:T(8,128)(2,1)S(1)}, bf16[144,256]{1,0:T(8,128)(2,1)S(1)}, u32[]{:S(2)}, u32[]{:S(2)}) %collective-permute-start.9) | collective-permute-done | bytes 73760 | tf_op jit(solution)/shard_map/ppermute | solution.py:26
  110.6 0.0 collective-permute-done.10.r3
  110.7 0.0 collective-permute-done.11.r2
  110.7 3.6 %collective-permute-start.12 = (bf16[256,256]{1,0:T(8,128)(2,1)S(1)}, bf16[256,256]{1,0:T(8,128)(2,1)S(1)}, u32[]{:S(2)}, u32[]{:S(2)}) collective-permute-start(bf16[256,256]{1,0:T(8,128)(2,1)S(1)} %pad_maximum_fusion.4), channel_id=1, source_target_pairs={{0,32},{32,0},{64,96},{96,64},{1,33},{33,1},{65,97},{97,65},{2,34}... | collective-permute-start | bytes 393224 | tf_op jit(solution)/shard_map/ppermute | solution.py:26
  114.3 0.1 shard_map.62
  114.4 6.4 %collective-permute-start.17 = (bf16[64,256]{1,0:T(8,128)(2,1)S(1)}, bf16[64,256]{1,0:T(8,128)(2,1)S(1)}, u32[]{:S(2)}, u32[]{:S(2)}) collective-permute-start(bf16[64,256]{1,0:T(8,128)(2,1)S(1)} %shard_map.62), channel_id=1, source_target_pairs={{0,128},{128,0},{256,384},{384,256},{1,129},{129,1},{257,385},{385... | collective-permute-start | bytes 98312 | tf_op jit(solution)/shard_map/ppermute | solution.py:26
  120.9 3.2 %collective-permute-done.17 = bf16[64,256]{1,0:T(8,128)(2,1)S(1)} collective-permute-done((bf16[64,256]{1,0:T(8,128)(2,1)S(1)}, bf16[64,256]{1,0:T(8,128)(2,1)S(1)}, u32[]{:S(2)}, u32[]{:S(2)}) %collective-permute-start.17) | collective-permute-done | bytes 32800 | tf_op jit(solution)/shard_map/ppermute | solution.py:26
  124.1 6.5 %collective-permute-start.18 = (bf16[128,256]{1,0:T(8,128)(2,1)S(1)}, bf16[128,256]{1,0:T(8,128)(2,1)S(1)}, u32[]{:S(2)}, u32[]{:S(2)}) collective-permute-start(bf16[128,256]{1,0:T(8,128)(2,1)S(1)} %pad_maximum_fusion.10), channel_id=1, source_target_pairs={{0,384},{128,256},{256,128},{384,0},{1,385},{129,257},{257,129},{3... | collective-permute-start | bytes 196616 | tf_op jit(solution)/shard_map/ppermute | solution.py:26
  130.7 0.0 collective-permute-done.12
  130.7 2.2 %collective-permute-start.13 = (bf16[512,256]{1,0:T(8,128)(2,1)S(1)}, bf16[512,256]{1,0:T(8,128)(2,1)S(1)}, u32[]{:S(2)}, u32[]{:S(2)}) collective-permute-start(bf16[512,256]{1,0:T(8,128)(2,1)S(1)} %constant_dynamic-update-slice_fusion.b0), channel_id=1, source_target_pairs={{0,96},{32,64},{64,32},{96,0},{1,97},{33,65},{65,33},{97,1},{2,98}... | collective-permute-start | bytes 786440 | tf_op jit(solution)/shard_map/ppermute | solution.py:26
  132.9 0.0 collective-permute-done.15
  132.9 4.8 %collective-permute-start.16 = (bf16[512,256]{1,0:T(8,128)(2,1)S(1)}, bf16[512,256]{1,0:T(8,128)(2,1)S(1)}, u32[]{:S(2)}, u32[]{:S(2)}) collective-permute-start(bf16[512,256]{1,0:T(8,128)(2,1)S(1)} %constant_dynamic-update-slice_fusion.5.t0), channel_id=1, source_target_pairs={{0,96},{32,64},{64,32},{96,0},{1,97},{33,65},{65,33},{97,1},{2,98}... | collective-permute-start | bytes 786440 | tf_op jit(solution)/shard_map/ppermute | solution.py:26
  137.8 0.0 collective-permute-done.18
  137.8 1.9 %collective-permute-start.19 = (bf16[256,256]{1,0:T(8,128)(2,1)S(1)}, bf16[256,256]{1,0:T(8,128)(2,1)S(1)}, u32[]{:S(2)}, u32[]{:S(2)}) collective-permute-start(bf16[256,256]{1,0:T(8,128)(2,1)S(1)} %pad_maximum_fusion.6.c0), channel_id=1, source_target_pairs={{0,32},{32,0},{64,96},{96,64},{1,33},{33,1},{65,97},{97,65},{2,34}... | collective-permute-start | bytes 393224 | tf_op jit(solution)/shard_map/ppermute | solution.py:26
  139.7 3.0 %collective-permute-start.20 = (bf16[256,256]{1,0:T(8,128)(2,1)S(1)}, bf16[256,256]{1,0:T(8,128)(2,1)S(1)}, u32[]{:S(2)}, u32[]{:S(2)}) collective-permute-start(bf16[256,256]{1,0:T(8,128)(2,1)S(1)} %pad_maximum_fusion.6.c0), channel_id=1, source_target_pairs={{0,96},{32,64},{64,32},{96,0},{1,97},{33,65},{65,33},{97,1},{2,98}... | collective-permute-start | bytes 393224 | tf_op jit(solution)/shard_map/ppermute | solution.py:26
  142.8 4.9 %collective-permute-start.21 = (bf16[256,256]{1,0:T(8,128)(2,1)S(1)}, bf16[256,256]{1,0:T(8,128)(2,1)S(1)}, u32[]{:S(2)}, u32[]{:S(2)}) collective-permute-start(bf16[256,256]{1,0:T(8,128)(2,1)S(1)} %pad_maximum_fusion.6.c0), channel_id=1, source_target_pairs={{0,64},{32,96},{64,0},{96,32},{1,65},{33,97},{65,1},{97,33},{2,66}... | collective-permute-start | bytes 393224 | tf_op jit(solution)/shard_map/ppermute | solution.py:26
  147.7 0.0 collective-permute-done.13.b1
  147.7 9.5 %shard_map.60.inverse = f32[256,256]{1,0:T(8,128)S(1)} custom-call(bf16[512,256]{1,0:T(8,128)(2,1)S(1)} %constant_dynamic-update-slice_fusion.b0, bf16[512,256]{1,0:T(8,128)(2,1)S(1)} %collective-permute-done.13.b1), custom_call_target="tpu_custom_call" | custom-call | tf_op jit(solution)/shard_map/pallas_call | solution.py:47
  157.1 0.0 collective-permute-done.16.t1
  157.2 1.6 %shard_map.61 = f32[256,256]{1,0:T(8,128)} custom-call(s32[1]{0:T(128)} %bitcast.1.is_band, bf16[512,256]{1,0:T(8,128)(2,1)S(1)} %constant_dynamic-update-slice_fusion.b0, bf16[512,256]{1,0:T(8,128)(2,1)S(1)} %collective-permute-done.13.b1, bf16[512,256]{1,0:T(8,128)(2,1)S(1)} %constant_dynamic-update-slice_fusion.5.t0, ...), custom_call_target="tpu_custom_call" | custom-call | tf_op jit(solution)/shard_map/pallas_call | solution.py:47
  158.8 1.6 %shard_map.63 = f32[256,256]{1,0:T(8,128)} custom-call(bf16[512,256]{1,0:T(8,128)(2,1)S(1)} %constant_dynamic-update-slice_fusion.b0, bf16[512,256]{1,0:T(8,128)(2,1)S(1)} %collective-permute-done.13.b1, bf16[256,256]{1,0:T(8,128)(2,1)S(1)} %pad_maximum_fusion.6.c0, bf16[256,256]{1,0:T(8,128)(2,1)S(1)} %collective-permute-done.19.c1, ...), custom_call_target="tpu_custom_call" | custom-call | tf_op jit(solution)/shard_map/pallas_call | solution.py:47
  (35 shorter events, 0.3 us)
Async XLA Ops:
  0.6 15.6 %collective-permute-start = (bf16[64,256]{1,0:T(8,128)(2,1)}, bf16[64,256]{1,0:T(8,128)(2,1)S(1)}, u32[]{:S(2)}, u32[]{:S(2)}) collective-permute-start(bf16[64,256]{1,0:T(8,128)(2,1)} %tokens.1), channel_id=1, source_target_pairs={{0,0},{1,1},{2,2},{3,3},{4,4},{5,5},{6,6},{7,7},{8,128},{9,129},{1... | collective-permute-start | bytes 98312 | tf_op jit(solution)/shard_map/ppermute | solution.py:178
  16.2 25.7 %copy-start.1 = (bf16[64,256]{1,0:T(8,128)(2,1)S(1)}, bf16[64,256]{1,0:T(8,128)(2,1)}, u32[]{:S(2)}) copy-start(bf16[64,256]{1,0:T(8,128)(2,1)} %tokens.1) | copy-start | bytes 98308
  16.2 7.1 %collective-permute-start.1 = (bf16[128,256]{1,0:T(8,128)(2,1)S(1)}, bf16[128,256]{1,0:T(8,128)(2,1)S(1)}, u32[]{:S(2)}, u32[]{:S(2)}) collective-permute-start(bf16[128,256]{1,0:T(8,128)(2,1)S(1)} %pad_maximum_fusion.8), channel_id=1, source_target_pairs={{0,2},{2,0},{4,6},{6,4},{1,3},{3,1},{5,7},{7,5},{8,10},{10,8},{12,... | collective-permute-start | bytes 196616 | tf_op jit(solution)/shard_map/ppermute | solution.py:26
  18.4 9.0 %collective-permute-start.2 = (bf16[512,256]{1,0:T(8,128)(2,1)}, bf16[512,256]{1,0:T(8,128)(2,1)S(1)}, u32[]{:S(2)}, u32[]{:S(2)}) collective-permute-start(bf16[512,256]{1,0:T(8,128)(2,1)} %p0), channel_id=1, source_target_pairs={{0,32},{32,0},{64,96},{96,64},{1,33},{33,1},{65,97},{97,65},{2,34}... | collective-permute-start | bytes 786440 | tf_op jit(solution)/shard_map/ppermute | solution.py:26
  27.4 8.5 %collective-permute-start.3 = (bf16[192,256]{1,0:T(8,128)(2,1)S(1)}, bf16[192,256]{1,0:T(8,128)(2,1)S(1)}, u32[]{:S(2)}, u32[]{:S(2)}) collective-permute-start(bf16[192,256]{1,0:T(8,128)(2,1)S(1)} %pad_maximum_fusion.7), channel_id=1, source_target_pairs={{0,4},{2,6},{4,0},{6,2},{1,5},{3,7},{5,1},{7,3},{8,12},{10,14},{12... | collective-permute-start | bytes 294920 | tf_op jit(solution)/shard_map/ppermute | solution.py:26
  35.9 16.2 %collective-permute-start.4 = (bf16[320,256]{1,0:T(8,128)(2,1)S(1)}, bf16[320,256]{1,0:T(8,128)(2,1)S(1)}, u32[]{:S(2)}, u32[]{:S(2)}) collective-permute-start(bf16[320,256]{1,0:T(8,128)(2,1)S(1)} %pad_maximum_fusion.3), channel_id=1, source_target_pairs={{0,8},{8,0},{16,24},{24,16},{1,9},{9,1},{17,25},{25,17},{2,10},{10... | collective-permute-start | bytes 491528 | tf_op jit(solution)/shard_map/ppermute | solution.py:26
  41.9 10.2 %collective-permute-start.5 = (bf16[64,256]{1,0:T(8,128)(2,1)S(1)}, bf16[64,256]{1,0:T(8,128)(2,1)S(1)}, u32[]{:S(2)}, u32[]{:S(2)}) collective-permute-start(bf16[64,256]{1,0:T(8,128)(2,1)S(1)} %copy-done.1), channel_id=1, source_target_pairs={{0,128},{128,0},{256,384},{384,256},{1,129},{129,1},{257,385},{385... | collective-permute-start | bytes 98312 | tf_op jit(solution)/shard_map/ppermute | solution.py:26
  52.2 9.8 %collective-permute-start.6 = (bf16[576,256]{1,0:T(8,128)(2,1)S(1)}, bf16[576,256]{1,0:T(8,128)(2,1)S(1)}, u32[]{:S(2)}, u32[]{:S(2)}) collective-permute-start(bf16[576,256]{1,0:T(8,128)(2,1)S(1)} %pad_maximum_fusion.2), channel_id=1, source_target_pairs={{0,24},{8,16},{16,8},{24,0},{1,25},{9,17},{17,9},{25,1},{2,26},{10... | collective-permute-start | bytes 884744 | tf_op jit(solution)/shard_map/ppermute | solution.py:26
  62.0 2.1 %copy-start = (bf16[512,256]{1,0:T(8,128)(2,1)S(1)}, bf16[512,256]{1,0:T(8,128)(2,1)}, u32[]{:S(2)}) copy-start(bf16[512,256]{1,0:T(8,128)(2,1)} %p0) | copy-start | bytes 786436
  62.1 23.5 %collective-permute-start.7 = (bf16[1088,256]{1,0:T(8,128)(2,1)S(1)}, bf16[1088,256]{1,0:T(8,128)(2,1)S(1)}, u32[]{:S(2)}, u32[]{:S(2)}) collective-permute-start(bf16[1088,256]{1,0:T(8,128)(2,1)S(1)} %pad_maximum_fusion.mine), channel_id=1, source_target_pairs={{0,1},{1,0},{2,3},{3,2},{4,5},{5,4},{6,7},{7,6},{8,9},{9,8},{10,11... | collective-permute-start | bytes 1671176 | tf_op jit(solution)/shard_map/ppermute | solution.py:26
  64.2 21.4 %collective-permute-start.8 = (bf16[1024,256]{1,0:T(8,128)(2,1)S(1)}, bf16[1024,256]{1,0:T(8,128)(2,1)S(1)}, u32[]{:S(2)}, u32[]{:S(2)}) collective-permute-start(bf16[1024,256]{1,0:T(8,128)(2,1)S(1)} %pad_maximum_fusion.1), channel_id=1, source_target_pairs={{0,96},{32,64},{64,32},{96,0},{1,97},{33,65},{65,33},{97,1},{2,98}... | collective-permute-start | bytes 1572872 | tf_op jit(solution)/shard_map/ppermute | solution.py:26
  69.1 14.4 %collective-permute-start.14 = (bf16[128,256]{1,0:T(8,128)(2,1)S(1)}, bf16[128,256]{1,0:T(8,128)(2,1)S(1)}, u32[]{:S(2)}, u32[]{:S(2)}) collective-permute-start(bf16[128,256]{1,0:T(8,128)(2,1)S(1)} %pad_maximum_fusion.9), channel_id=1, source_target_pairs={{0,384},{128,256},{256,128},{384,0},{1,385},{129,257},{257,129},{3... | collective-permute-start | bytes 196616 | tf_op jit(solution)/shard_map/ppermute | solution.py:26
  83.6 49.4 %collective-permute-start.15 = (bf16[256,256]{1,0:T(8,128)(2,1)S(1)}, bf16[256,256]{1,0:T(8,128)(2,1)S(1)}, u32[]{:S(2)}, u32[]{:S(2)}) collective-permute-start(bf16[256,256]{1,0:T(8,128)(2,1)S(1)} %pad_maximum_fusion.5), channel_id=1, source_target_pairs={{0,32},{32,0},{64,96},{96,64},{1,33},{33,1},{65,97},{97,65},{2,34}... | collective-permute-start | bytes 393224 | tf_op jit(solution)/shard_map/ppermute | solution.py:26
  86.2 24.5 %collective-permute-start.11 = (bf16[144,256]{1,0:T(8,128)(2,1)S(1)}, bf16[144,256]{1,0:T(8,128)(2,1)S(1)}, u32[]{:S(2)}, u32[]{:S(2)}) collective-permute-start(bf16[144,256]{1,0:T(8,128)(2,1)S(1)} %get-tuple-element.21), channel_id=1, source_target_pairs={{0,256},{128,384},{256,0},{384,128},{1,257},{129,385},{257,1},{385... | collective-permute-start | bytes 221192 | tf_op jit(solution)/shard_map/ppermute | solution.py:26
  93.0 17.6 %collective-permute-start.10 = (bf16[144,256]{1,0:T(8,128)(2,1)S(1)}, bf16[144,256]{1,0:T(8,128)(2,1)S(1)}, u32[]{:S(2)}, u32[]{:S(2)}) collective-permute-start(bf16[144,256]{1,0:T(8,128)(2,1)S(1)} %get-tuple-element.20), channel_id=1, source_target_pairs={{0,384},{128,256},{256,128},{384,0},{1,385},{129,257},{257,129},{3... | collective-permute-start | bytes 221192 | tf_op jit(solution)/shard_map/ppermute | solution.py:26
  100.2 10.4 %collective-permute-start.9 = (bf16[144,256]{1,0:T(8,128)(2,1)S(1)}, bf16[144,256]{1,0:T(8,128)(2,1)S(1)}, u32[]{:S(2)}, u32[]{:S(2)}) collective-permute-start(bf16[144,256]{1,0:T(8,128)(2,1)S(1)} %get-tuple-element.19), channel_id=1, source_target_pairs={{0,128},{128,0},{256,384},{384,256},{1,129},{129,1},{257,385},{385... | collective-permute-start | bytes 221192 | tf_op jit(solution)/shard_map/ppermute | solution.py:26
  110.7 20.0 %collective-permute-start.12 = (bf16[256,256]{1,0:T(8,128)(2,1)S(1)}, bf16[256,256]{1,0:T(8,128)(2,1)S(1)}, u32[]{:S(2)}, u32[]{:S(2)}) collective-permute-start(bf16[256,256]{1,0:T(8,128)(2,1)S(1)} %pad_maximum_fusion.4), channel_id=1, source_target_pairs={{0,32},{32,0},{64,96},{96,64},{1,33},{33,1},{65,97},{97,65},{2,34}... | collective-permute-start | bytes 393224 | tf_op jit(solution)/shard_map/ppermute | solution.py:26
  114.4 9.7 %collective-permute-start.17 = (bf16[64,256]{1,0:T(8,128)(2,1)S(1)}, bf16[64,256]{1,0:T(8,128)(2,1)S(1)}, u32[]{:S(2)}, u32[]{:S(2)}) collective-permute-start(bf16[64,256]{1,0:T(8,128)(2,1)S(1)} %shard_map.62), channel_id=1, source_target_pairs={{0,128},{128,0},{256,384},{384,256},{1,129},{129,1},{257,385},{385... | collective-permute-start | bytes 98312 | tf_op jit(solution)/shard_map/ppermute | solution.py:26
  124.1 13.7 %collective-permute-start.18 = (bf16[128,256]{1,0:T(8,128)(2,1)S(1)}, bf16[128,256]{1,0:T(8,128)(2,1)S(1)}, u32[]{:S(2)}, u32[]{:S(2)}) collective-permute-start(bf16[128,256]{1,0:T(8,128)(2,1)S(1)} %pad_maximum_fusion.10), channel_id=1, source_target_pairs={{0,384},{128,256},{256,128},{384,0},{1,385},{129,257},{257,129},{3... | collective-permute-start | bytes 196616 | tf_op jit(solution)/shard_map/ppermute | solution.py:26
  130.7 17.0 %collective-permute-start.13 = (bf16[512,256]{1,0:T(8,128)(2,1)S(1)}, bf16[512,256]{1,0:T(8,128)(2,1)S(1)}, u32[]{:S(2)}, u32[]{:S(2)}) collective-permute-start(bf16[512,256]{1,0:T(8,128)(2,1)S(1)} %constant_dynamic-update-slice_fusion.b0), channel_id=1, source_target_pairs={{0,96},{32,64},{64,32},{96,0},{1,97},{33,65},{65,33},{97,1},{2,98}... | collective-permute-start | bytes 786440 | tf_op jit(solution)/shard_map/ppermute | solution.py:26
  132.9 24.2 %collective-permute-start.16 = (bf16[512,256]{1,0:T(8,128)(2,1)S(1)}, bf16[512,256]{1,0:T(8,128)(2,1)S(1)}, u32[]{:S(2)}, u32[]{:S(2)}) collective-permute-start(bf16[512,256]{1,0:T(8,128)(2,1)S(1)} %constant_dynamic-update-slice_fusion.5.t0), channel_id=1, source_target_pairs={{0,96},{32,64},{64,32},{96,0},{1,97},{33,65},{65,33},{97,1},{2,98}... | collective-permute-start | bytes 786440 | tf_op jit(solution)/shard_map/ppermute | solution.py:26
  137.8 21.0 %collective-permute-start.19 = (bf16[256,256]{1,0:T(8,128)(2,1)S(1)}, bf16[256,256]{1,0:T(8,128)(2,1)S(1)}, u32[]{:S(2)}, u32[]{:S(2)}) collective-permute-start(bf16[256,256]{1,0:T(8,128)(2,1)S(1)} %pad_maximum_fusion.6.c0), channel_id=1, source_target_pairs={{0,32},{32,0},{64,96},{96,64},{1,33},{33,1},{65,97},{97,65},{2,34}... | collective-permute-start | bytes 393224 | tf_op jit(solution)/shard_map/ppermute | solution.py:26
  139.7 19.0 %collective-permute-start.20 = (bf16[256,256]{1,0:T(8,128)(2,1)S(1)}, bf16[256,256]{1,0:T(8,128)(2,1)S(1)}, u32[]{:S(2)}, u32[]{:S(2)}) collective-permute-start(bf16[256,256]{1,0:T(8,128)(2,1)S(1)} %pad_maximum_fusion.6.c0), channel_id=1, source_target_pairs={{0,96},{32,64},{64,32},{96,0},{1,97},{33,65},{65,33},{97,1},{2,98}... | collective-permute-start | bytes 393224 | tf_op jit(solution)/shard_map/ppermute | solution.py:26
  142.8 16.0 %collective-permute-start.21 = (bf16[256,256]{1,0:T(8,128)(2,1)S(1)}, bf16[256,256]{1,0:T(8,128)(2,1)S(1)}, u32[]{:S(2)}, u32[]{:S(2)}) collective-permute-start(bf16[256,256]{1,0:T(8,128)(2,1)S(1)} %pad_maximum_fusion.6.c0), channel_id=1, source_target_pairs={{0,64},{32,96},{64,0},{96,32},{1,65},{33,97},{65,1},{97,33},{2,66}... | collective-permute-start | bytes 393224 | tf_op jit(solution)/shard_map/ppermute | solution.py:26
where the time goes:
time: 163 us; the launch traced here: 160 us
  starting transfers between devices  108 us (66%)
  waiting for transfers between devices  36.3 us (22%)
  Pallas kernels  13.4 us (8%)
  between operations  1.76 us (1%)
    ppermute x21, starting transfers between devices, swap(): return lax.ppermute(value, axis, [(i, i ^ bits) for i in range(size)])  95.2 us
    ppermute x21, waiting for transfers between devices, swap(): return lax.ppermute(value, axis, [(i, i ^ bits) for i in range(size)])  34.8 us
    pallas_call x5, Pallas kernels, call(): pl.pallas_call(kernel, out_shape=outs, in_specs=[smem] * n_scalars + [vme...  13.4 us
    ppermute x1, starting transfers between devices, steps(): lax.ppermute(tokens, AXES, [(((a * 4 + b) * 4 + d) * 8 + e, ((d * 4 + b)...  12.7 us
  transfers between devices with their start and end apart: 22, of which 9 were waited for; matrix products, arithmetic and copies ran while one was open for 1% of the time, Pallas kernels for 7%

commit v1 on v0

--- a/solution.py
+++ b/solution.py
@@ -16,7 +16,7 @@
 TOK = ("zh", "y")
 FEAT = ("x", "zl", "c")
 NB = 64
-STEP = 8
+STEP = 16
 F32 = jnp.float32
 BF16 = jnp.bfloat16
 HIGHEST = lax.Precision.HIGHEST
@@ -30,8 +30,11 @@
     return jnp.concatenate([value, swap(value, axis, bits)], axis=0)
 
 
-def merge(mine, other):
-    return jnp.concatenate([mine[:64] + other[:64], mine[64:], other[64:]], axis=0)
+def spread(load, axis):
+    parts = jnp.broadcast_to(load[None], (4, *load.shape))
+    parts = lax.all_to_all(parts, axis, 0, 0, tiled=True)
+    band = parts[0, :64] + parts[1, :64] + parts[2, :64] + parts[3, :64]
+    return jnp.concatenate([band] + [parts[i, 64:] for i in range(4)], axis=0), band
 
 
 def call(kernel, outs, *args, n_scalars=0, scratch=(), final=False):
@@ -57,31 +60,30 @@
     return lax.dot_general(a, b, (((0,), (0,)), ((), ())), preferred_element_type=F32)
 
 
-def project_kernel(mine, other, gain, p0, p1, far, keep, s1, s2, s3, acc, sq):
-    zh, y, x, zl, c = [lax.axis_index(a) for a in AXES]
+def project_kernel(mine, other, gain, p0, p1, p2, p3, keep, s1, s2, s3, acc, sq):
+    zh, y, c = [lax.axis_index(a) for a in ("zh", "y", "c")]
     total = jnp.zeros((256, 256), F32)
     squares = jnp.zeros((256, 256), F32)
-    for y_rel, (proj, at) in enumerate(((p0, 0), (p1, 0), (far, 512), (far, 0))):
+    for y_rel, proj in enumerate((p0, p1, p2, p3)):
         zl_there = y ^ y_rel
-        z_rel = zl ^ zl_there
         for c_rel, src in enumerate((mine, other)):
             c_there = c ^ c_rel
             rows = [
-                src[pl.ds(pl.multiple_of(64 + (at_x * 4 + z_rel) * 64, 64), 64), :]
-                for at_x in (0, 1, 3, 2)
+                src[pl.ds(pl.multiple_of(64 + (at_x * 4 + zl_there) * 64, 64), 64), :]
+                for at_x in range(4)
             ]
             raw = jnp.concatenate(rows, axis=0).astype(F32)
             squares = squares + raw * raw
             scale = gain[pl.ds(8 * zh + 2 * zl_there + c_there, 1), :]
             scaled = (raw * scale).astype(BF16)
-            weights = proj[pl.ds(pl.multiple_of(at + c_there * 256, 256), 256), :]
+            weights = proj[pl.ds(pl.multiple_of(c_there * 256, 256), 256), :]
             total = total + jnp.dot(scaled, weights, preferred_element_type=F32)
     acc[...] = total
     sq[...] = jnp.broadcast_to(jnp.sum(squares, axis=1, keepdims=True), (256, 256))
     row = lax.broadcasted_iota(jnp.int32, (64, 256), 0)
     lane = lax.broadcasted_iota(jnp.int32, (64, 256), 1)
     for step, out in enumerate((keep, s1, s2, s3)):
-        at = pl.multiple_of((x ^ zh ^ step) * 64, 64)
+        at = pl.multiple_of((zh ^ step) * 64, 64)
         part = acc[pl.ds(at, 64), :]
         norm = sq[pl.ds(at, 64), :]
         high = norm.astype(BF16).astype(F32)
@@ -186,21 +188,15 @@
             for e in range(8)
         ],
     )
-    weights = [proj, swap(proj, "y", 1)]
+    weights = [proj] + [swap(proj, "y", k) for k in (1, 2, 3)]
 
     load = jnp.concatenate([band, turned], axis=0)
     load, gains = lax.optimization_barrier((load, gains))
-    load = merge(load, swap(load, "zl", 1))
-    load, weights = lax.optimization_barrier((load, weights))
-    weights.append(swap(jnp.concatenate(weights, axis=0), "y", 3))
-    load = merge(load, swap(load, "zl", 2))
-    there = swap(load, "x", 1)
-    blocks = double(tokens, "zh", 1)
-    load, blocks = lax.optimization_barrier((merge(load, there), blocks))
-    there = swap(load, "x", 3)
+    load, band = spread(load, "zl")
+    load, early = lax.optimization_barrier((load, tokens))
+    blocks = double(early, "zh", 1)
+    load, band = spread(load, "x")
     blocks = double(blocks, "zh", 3)
-    load = merge(load, there)
-    band = load[:64]
     other = swap(load, "c", 1, 2)
     band = band + other[:64]
 

time: 163 us -> 158 us (0.969)
  blocking collectives: 0 us -> 26.4 us
  waiting for transfers between devices: 36.3 us -> 18.2 us
  starting transfers between devices: 108 us -> 95.5 us
    all_to_all x0 -> x2, blocking collectives: none -> 26.4 us  [spread(): parts = lax.all_to_all(parts, axis, 0, 0, tiled=True)]
    ppermute x21 -> x18, waiting for transfers between devices: 34.8 us -> 16.7 us  [swap(): return lax.ppermute(value, axis, [(i, i ^ bits) for i in range(size)])]
    ppermute x21 -> x18, starting transfers between devices: 95.2 us -> 82.8 us  [swap(): return lax.ppermute(value, axis, [(i, i ^ bits) for i in range(size)])]
  transfers between devices with their start and end apart: 22 -> 19, of which waited for: 9 -> 6; matrix products, arithmetic and copies ran while one was open for 1% -> 0% of each run, Pallas kernels for 7% -> 7%
where the time goes in v1:
time: 158 us; the launch traced here: 155 us
  starting transfers between devices  95.5 us (60%)
  blocking collectives  26.4 us (17%)
  waiting for transfers between devices  18.2 us (12%)
  Pallas kernels  12.2 us (8%)
  between operations  1.76 us (1%)
    ppermute x18, starting transfers between devices, swap(): return lax.ppermute(value, axis, [(i, i ^ bits) for i in range(size)])  82.8 us
    all_to_all x2, blocking collectives, spread(): parts = lax.all_to_all(parts, axis, 0, 0, tiled=True)  26.4 us
    ppermute x18, waiting for transfers between devices, swap(): return lax.ppermute(value, axis, [(i, i ^ bits) for i in range(size)])  16.7 us
    ppermute x1, starting transfers between devices, steps(): lax.ppermute(tokens, AXES, [(((a * 4 + b) * 4 + d) * 8 + e, ((d * 4 + b)...  12.7 us
    pallas_call x5, Pallas kernels, call(): pl.pallas_call(kernel, out_shape=outs, in_specs=[smem] * n_scalars + [vme...  12.2 us
  transfers between devices with their start and end apart: 19, of which 6 were waited for; matrix products, arithmetic and copies ran while one was open for 0% of the time, Pallas kernels for 7%

profile of v1, /device:TPU:6, one launch (start us, length us, event | category | flops | bytes accessed | tf_op | source)
XLA Modules:
  0.0 155.0 jit_solution(5010414813865009070)
XLA Ops:
  0.6 12.7 %collective-permute-start = (bf16[64,256]{1,0:T(8,128)(2,1)}, bf16[64,256]{1,0:T(8,128)(2,1)S(1)}, u32[]{:S(2)}, u32[]{:S(2)}) collective-permute-start(bf16[64,256]{1,0:T(8,128)(2,1)} %tokens.1), channel_id=1, source_target_pairs={{0,0},{1,1},{2,2},{3,3},{4,4},{5,5},{6,6},{7,7},{8,128},{9,129},{1... | collective-permute-start | bytes 98312 | tf_op jit(solution)/shard_map/ppermute | solution.py:180
  14.0 0.7 copy-done.2
  14.7 1.5 collective-permute-done
  16.3 11.0 %all_to_all.10 = bf16[4,128,256]{2,1,0:T(8,128)(2,1)S(1)} all-to-all(bf16[4,128,256]{2,1,0:T(8,128)(2,1)S(1)} %broadcast_in_dim.7), channel_id=1, replica_groups=mesh['zh'=4,'y'=4,'x'=4,'zl'=4,'c'=2] {'zl'}, dimensions={0} | all-to-all | bytes 524288 | tf_op jit(solution)/shard_map/all_to_all | solution.py:35
  27.4 15.3 %all_to_all.11 = bf16[4,320,256]{2,1,0:T(8,128)(2,1)S(1)} all-to-all(bf16[4,320,256]{2,1,0:T(8,128)(2,1)S(1)} %broadcast_in_dim.8), channel_id=1, replica_groups=mesh['zh'=4,'y'=4,'x'=4,'zl'=4,'c'=2] {'x'}, dimensions={0} | all-to-all | bytes 1310720 | tf_op jit(solution)/shard_map/all_to_all | solution.py:35
  42.8 0.0 copy-start.1
  42.8 0.0 copy-start
  42.9 2.1 %collective-permute-start.1 = (bf16[1088,256]{1,0:T(8,128)(2,1)S(1)}, bf16[1088,256]{1,0:T(8,128)(2,1)S(1)}, u32[]{:S(2)}, u32[]{:S(2)}) collective-permute-start(bf16[1088,256]{1,0:T(8,128)(2,1)S(1)} %fusion.mine), channel_id=1, source_target_pairs={{0,1},{1,0},{2,3},{3,2},{4,5},{5,4},{6,7},{7,6},{8,9},{9,8},{10,11... | collective-permute-start | bytes 1671176 | tf_op jit(solution)/shard_map/ppermute | solution.py:26
  44.9 3.5 %collective-permute-start.2 = (bf16[512,256]{1,0:T(8,128)(2,1)S(1)}, bf16[512,256]{1,0:T(8,128)(2,1)S(1)}, u32[]{:S(2)}, u32[]{:S(2)}) collective-permute-start(bf16[512,256]{1,0:T(8,128)(2,1)S(1)} %copy-done.1), channel_id=1, source_target_pairs={{0,32},{32,0},{64,96},{96,64},{1,33},{33,1},{65,97},{97,65},{2,34}... | collective-permute-start | bytes 786440 | tf_op jit(solution)/shard_map/ppermute | solution.py:26
  48.4 4.8 %collective-permute-start.3 = (bf16[512,256]{1,0:T(8,128)(2,1)S(1)}, bf16[512,256]{1,0:T(8,128)(2,1)S(1)}, u32[]{:S(2)}, u32[]{:S(2)}) collective-permute-start(bf16[512,256]{1,0:T(8,128)(2,1)S(1)} %copy-done.1), channel_id=1, source_target_pairs={{0,64},{32,96},{64,0},{96,32},{1,65},{33,97},{65,1},{97,33},{2,66}... | collective-permute-start | bytes 786440 | tf_op jit(solution)/shard_map/ppermute | solution.py:26
  53.2 2.1 %collective-permute-start.4 = (bf16[512,256]{1,0:T(8,128)(2,1)S(1)}, bf16[512,256]{1,0:T(8,128)(2,1)S(1)}, u32[]{:S(2)}, u32[]{:S(2)}) collective-permute-start(bf16[512,256]{1,0:T(8,128)(2,1)S(1)} %copy-done.1), channel_id=1, source_target_pairs={{0,96},{32,64},{64,32},{96,0},{1,97},{33,65},{65,33},{97,1},{2,98}... | collective-permute-start | bytes 786440 | tf_op jit(solution)/shard_map/ppermute | solution.py:26
  55.4 8.8 %collective-permute-start.10 = (bf16[64,256]{1,0:T(8,128)(2,1)S(1)}, bf16[64,256]{1,0:T(8,128)(2,1)S(1)}, u32[]{:S(2)}, u32[]{:S(2)}) collective-permute-start(bf16[64,256]{1,0:T(8,128)(2,1)S(1)} %copy-done), channel_id=1, source_target_pairs={{0,128},{128,0},{256,384},{384,256},{1,129},{129,1},{257,385},{385... | collective-permute-start | bytes 98312 | tf_op jit(solution)/shard_map/ppermute | solution.py:26
  64.2 2.2 %collective-permute-done.10 = bf16[64,256]{1,0:T(8,128)(2,1)S(1)} collective-permute-done((bf16[64,256]{1,0:T(8,128)(2,1)S(1)}, bf16[64,256]{1,0:T(8,128)(2,1)S(1)}, u32[]{:S(2)}, u32[]{:S(2)}) %collective-permute-start.10) | collective-permute-done | bytes 32800 | tf_op jit(solution)/shard_map/ppermute | solution.py:26
  66.4 7.2 %collective-permute-start.11 = (bf16[128,256]{1,0:T(8,128)(2,1)S(1)}, bf16[128,256]{1,0:T(8,128)(2,1)S(1)}, u32[]{:S(2)}, u32[]{:S(2)}) collective-permute-start(bf16[128,256]{1,0:T(8,128)(2,1)S(1)} %pad_maximum_fusion.4), channel_id=1, source_target_pairs={{0,384},{128,256},{256,128},{384,0},{1,385},{129,257},{257,129},{3... | collective-permute-start | bytes 196616 | tf_op jit(solution)/shard_map/ppermute | solution.py:26
  73.7 3.9 %collective-permute-done.11 = bf16[128,256]{1,0:T(8,128)(2,1)S(1)} collective-permute-done((bf16[128,256]{1,0:T(8,128)(2,1)S(1)}, bf16[128,256]{1,0:T(8,128)(2,1)S(1)}, u32[]{:S(2)}, u32[]{:S(2)}) %collective-permute-start.11) | collective-permute-done | bytes 65568 | tf_op jit(solution)/shard_map/ppermute | solution.py:26
  77.6 2.2 %collective-permute-start.12 = (bf16[256,256]{1,0:T(8,128)(2,1)S(1)}, bf16[256,256]{1,0:T(8,128)(2,1)S(1)}, u32[]{:S(2)}, u32[]{:S(2)}) collective-permute-start(bf16[256,256]{1,0:T(8,128)(2,1)S(1)} %pad_maximum_fusion.1), channel_id=1, source_target_pairs={{0,32},{32,0},{64,96},{96,64},{1,33},{33,1},{65,97},{97,65},{2,34}... | collective-permute-start | bytes 393224 | tf_op jit(solution)/shard_map/ppermute | solution.py:26
  79.8 0.0 collective-permute-done.2.p1
  79.8 0.0 collective-permute-done.3.p2
  79.8 0.0 collective-permute-done.4.p3
  79.8 0.0 collective-permute-done.1.other
  79.8 0.6 shard_map.59
  80.4 9.2 %collective-permute-start.5 = (bf16[144,256]{1,0:T(8,128)(2,1)S(1)}, bf16[144,256]{1,0:T(8,128)(2,1)S(1)}, u32[]{:S(2)}, u32[]{:S(2)}) collective-permute-start(bf16[144,256]{1,0:T(8,128)(2,1)S(1)} %get-tuple-element.13), channel_id=1, source_target_pairs={{0,128},{128,0},{256,384},{384,256},{1,129},{129,1},{257,385},{385... | collective-permute-start | bytes 221192 | tf_op jit(solution)/shard_map/ppermute | solution.py:26
  89.6 2.9 %collective-permute-start.6 = (bf16[144,256]{1,0:T(8,128)(2,1)S(1)}, bf16[144,256]{1,0:T(8,128)(2,1)S(1)}, u32[]{:S(2)}, u32[]{:S(2)}) collective-permute-start(bf16[144,256]{1,0:T(8,128)(2,1)S(1)} %get-tuple-element.14), channel_id=1, source_target_pairs={{0,384},{128,256},{256,128},{384,0},{1,385},{129,257},{257,129},{3... | collective-permute-start | bytes 221192 | tf_op jit(solution)/shard_map/ppermute | solution.py:26
  92.4 6.3 %collective-permute-start.7 = (bf16[144,256]{1,0:T(8,128)(2,1)S(1)}, bf16[144,256]{1,0:T(8,128)(2,1)S(1)}, u32[]{:S(2)}, u32[]{:S(2)}) collective-permute-start(bf16[144,256]{1,0:T(8,128)(2,1)S(1)} %get-tuple-element.15), channel_id=1, source_target_pairs={{0,256},{128,384},{256,0},{384,128},{1,257},{129,385},{257,1},{385... | collective-permute-start | bytes 221192 | tf_op jit(solution)/shard_map/ppermute | solution.py:26
  98.8 0.0 collective-permute-done.5.r1
  98.8 0.9 collective-permute-done.6.r3
  99.7 8.9 %collective-permute-done.7.r2 = bf16[144,256]{1,0:T(8,128)(2,1)S(1)} collective-permute-done((bf16[144,256]{1,0:T(8,128)(2,1)S(1)}, bf16[144,256]{1,0:T(8,128)(2,1)S(1)}, u32[]{:S(2)}, u32[]{:S(2)}) %collective-permute-start.7) | collective-permute-done | bytes 73760 | tf_op jit(solution)/shard_map/ppermute | solution.py:26
  108.6 0.1 shard_map.62
  108.7 5.3 %collective-permute-start.14 = (bf16[64,256]{1,0:T(8,128)(2,1)S(1)}, bf16[64,256]{1,0:T(8,128)(2,1)S(1)}, u32[]{:S(2)}, u32[]{:S(2)}) collective-permute-start(bf16[64,256]{1,0:T(8,128)(2,1)S(1)} %shard_map.62), channel_id=1, source_target_pairs={{0,128},{128,0},{256,384},{384,256},{1,129},{129,1},{257,385},{385... | collective-permute-start | bytes 98312 | tf_op jit(solution)/shard_map/ppermute | solution.py:26
  114.1 3.6 %collective-permute-start.8 = (bf16[256,256]{1,0:T(8,128)(2,1)S(1)}, bf16[256,256]{1,0:T(8,128)(2,1)S(1)}, u32[]{:S(2)}, u32[]{:S(2)}) collective-permute-start(bf16[256,256]{1,0:T(8,128)(2,1)S(1)} %pad_maximum_fusion), channel_id=1, source_target_pairs={{0,32},{32,0},{64,96},{96,64},{1,33},{33,1},{65,97},{97,65},{2,34}... | collective-permute-start | bytes 393224 | tf_op jit(solution)/shard_map/ppermute | solution.py:26
  117.7 0.7 collective-permute-done.14
  118.5 6.8 %collective-permute-start.15 = (bf16[128,256]{1,0:T(8,128)(2,1)S(1)}, bf16[128,256]{1,0:T(8,128)(2,1)S(1)}, u32[]{:S(2)}, u32[]{:S(2)}) collective-permute-start(bf16[128,256]{1,0:T(8,128)(2,1)S(1)} %pad_maximum_fusion.5), channel_id=1, source_target_pairs={{0,384},{128,256},{256,128},{384,0},{1,385},{129,257},{257,129},{3... | collective-permute-start | bytes 196616 | tf_op jit(solution)/shard_map/ppermute | solution.py:26
  125.2 0.0 collective-permute-done.8
  125.3 4.4 %collective-permute-start.9 = (bf16[512,256]{1,0:T(8,128)(2,1)S(1)}, bf16[512,256]{1,0:T(8,128)(2,1)S(1)}, u32[]{:S(2)}, u32[]{:S(2)}) collective-permute-start(bf16[512,256]{1,0:T(8,128)(2,1)S(1)} %constant_dynamic-update-slice_fusion.6.b0), channel_id=1, source_target_pairs={{0,96},{32,64},{64,32},{96,0},{1,97},{33,65},{65,33},{97,1},{2,98}... | collective-permute-start | bytes 786440 | tf_op jit(solution)/shard_map/ppermute | solution.py:26
  129.7 0.0 collective-permute-done.12
  129.7 2.6 %collective-permute-start.13 = (bf16[512,256]{1,0:T(8,128)(2,1)S(1)}, bf16[512,256]{1,0:T(8,128)(2,1)S(1)}, u32[]{:S(2)}, u32[]{:S(2)}) collective-permute-start(bf16[512,256]{1,0:T(8,128)(2,1)S(1)} %constant_dynamic-update-slice_fusion.11.t0), channel_id=1, source_target_pairs={{0,96},{32,64},{64,32},{96,0},{1,97},{33,65},{65,33},{97,1},{2,98}... | collective-permute-start | bytes 786440 | tf_op jit(solution)/shard_map/ppermute | solution.py:26
  132.4 0.0 collective-permute-done.15
  132.4 4.6 %collective-permute-start.16 = (bf16[256,256]{1,0:T(8,128)(2,1)S(1)}, bf16[256,256]{1,0:T(8,128)(2,1)S(1)}, u32[]{:S(2)}, u32[]{:S(2)}) collective-permute-start(bf16[256,256]{1,0:T(8,128)(2,1)S(1)} %pad_maximum_fusion.2.c0), channel_id=1, source_target_pairs={{0,32},{32,0},{64,96},{96,64},{1,33},{33,1},{65,97},{97,65},{2,34}... | collective-permute-start | bytes 393224 | tf_op jit(solution)/shard_map/ppermute | solution.py:26
  137.0 4.5 %collective-permute-start.17 = (bf16[256,256]{1,0:T(8,128)(2,1)S(1)}, bf16[256,256]{1,0:T(8,128)(2,1)S(1)}, u32[]{:S(2)}, u32[]{:S(2)}) collective-permute-start(bf16[256,256]{1,0:T(8,128)(2,1)S(1)} %pad_maximum_fusion.2.c0), channel_id=1, source_target_pairs={{0,96},{32,64},{64,32},{96,0},{1,97},{33,65},{65,33},{97,1},{2,98}... | collective-permute-start | bytes 393224 | tf_op jit(solution)/shard_map/ppermute | solution.py:26
  141.5 1.9 %collective-permute-start.18 = (bf16[256,256]{1,0:T(8,128)(2,1)S(1)}, bf16[256,256]{1,0:T(8,128)(2,1)S(1)}, u32[]{:S(2)}, u32[]{:S(2)}) collective-permute-start(bf16[256,256]{1,0:T(8,128)(2,1)S(1)} %pad_maximum_fusion.2.c0), channel_id=1, source_target_pairs={{0,64},{32,96},{64,0},{96,32},{1,65},{33,97},{65,1},{97,33},{2,66}... | collective-permute-start | bytes 393224 | tf_op jit(solution)/shard_map/ppermute | solution.py:26
  143.5 0.0 collective-permute-done.9.b1
  143.5 8.3 %shard_map.60.inverse = f32[256,256]{1,0:T(8,128)S(1)} custom-call(bf16[512,256]{1,0:T(8,128)(2,1)S(1)} %constant_dynamic-update-slice_fusion.6.b0, bf16[512,256]{1,0:T(8,128)(2,1)S(1)} %collective-permute-done.9.b1), custom_call_target="tpu_custom_call" | custom-call | tf_op jit(solution)/shard_map/pallas_call | solution.py:50
  151.8 0.0 collective-permute-done.13.t1
  151.8 1.6 %shard_map.61 = f32[256,256]{1,0:T(8,128)} custom-call(s32[1]{0:T(128)} %bitcast.1.is_band, bf16[512,256]{1,0:T(8,128)(2,1)S(1)} %constant_dynamic-update-slice_fusion.6.b0, bf16[512,256]{1,0:T(8,128)(2,1)S(1)} %collective-permute-done.9.b1, bf16[512,256]{1,0:T(8,128)(2,1)S(1)} %constant_dynamic-update-slice_fusion.11.t0, ...), custom_call_target="tpu_custom_call" | custom-call | tf_op jit(solution)/shard_map/pallas_call | solution.py:50
  153.4 0.0 collective-permute-done.16.c1
  153.4 0.0 collective-permute-done.17.c2
  153.4 0.0 collective-permute-done.18.c3
  153.4 1.6 %shard_map.63 = f32[256,256]{1,0:T(8,128)} custom-call(bf16[512,256]{1,0:T(8,128)(2,1)S(1)} %constant_dynamic-update-slice_fusion.6.b0, bf16[512,256]{1,0:T(8,128)(2,1)S(1)} %collective-permute-done.9.b1, bf16[256,256]{1,0:T(8,128)(2,1)S(1)} %pad_maximum_fusion.2.c0, bf16[256,256]{1,0:T(8,128)(2,1)S(1)} %collective-permute-done.16.c1, ...), custom_call_target="tpu_custom_call" | custom-call | tf_op jit(solution)/shard_map/pallas_call | solution.py:50
  (32 shorter events, 0.3 us)
Async XLA Ops:
  0.6 15.6 %collective-permute-start = (bf16[64,256]{1,0:T(8,128)(2,1)}, bf16[64,256]{1,0:T(8,128)(2,1)S(1)}, u32[]{:S(2)}, u32[]{:S(2)}) collective-permute-start(bf16[64,256]{1,0:T(8,128)(2,1)} %tokens.1), channel_id=1, source_target_pairs={{0,0},{1,1},{2,2},{3,3},{4,4},{5,5},{6,6},{7,7},{8,128},{9,129},{1... | collective-permute-start | bytes 98312 | tf_op jit(solution)/shard_map/ppermute | solution.py:180
  13.9 0.8 copy-start.2
  42.8 2.1 %copy-start.1 = (bf16[512,256]{1,0:T(8,128)(2,1)S(1)}, bf16[512,256]{1,0:T(8,128)(2,1)}, u32[]{:S(2)}) copy-start(bf16[512,256]{1,0:T(8,128)(2,1)} %p0.1) | copy-start | bytes 786436
  42.8 12.6 %copy-start = (bf16[64,256]{1,0:T(8,128)(2,1)S(1)}, bf16[64,256]{1,0:T(8,128)(2,1)}, u32[]{:S(2)}) copy-start(bf16[64,256]{1,0:T(8,128)(2,1)} %tokens.1) | copy-start | bytes 98308
  42.9 37.0 %collective-permute-start.1 = (bf16[1088,256]{1,0:T(8,128)(2,1)S(1)}, bf16[1088,256]{1,0:T(8,128)(2,1)S(1)}, u32[]{:S(2)}, u32[]{:S(2)}) collective-permute-start(bf16[1088,256]{1,0:T(8,128)(2,1)S(1)} %fusion.mine), channel_id=1, source_target_pairs={{0,1},{1,0},{2,3},{3,2},{4,5},{5,4},{6,7},{7,6},{8,9},{9,8},{10,11... | collective-permute-start | bytes 1671176 | tf_op jit(solution)/shard_map/ppermute | solution.py:26
  44.9 34.8 %collective-permute-start.2 = (bf16[512,256]{1,0:T(8,128)(2,1)S(1)}, bf16[512,256]{1,0:T(8,128)(2,1)S(1)}, u32[]{:S(2)}, u32[]{:S(2)}) collective-permute-start(bf16[512,256]{1,0:T(8,128)(2,1)S(1)} %copy-done.1), channel_id=1, source_target_pairs={{0,32},{32,0},{64,96},{96,64},{1,33},{33,1},{65,97},{97,65},{2,34}... | collective-permute-start | bytes 786440 | tf_op jit(solution)/shard_map/ppermute | solution.py:26
  48.4 31.4 %collective-permute-start.3 = (bf16[512,256]{1,0:T(8,128)(2,1)S(1)}, bf16[512,256]{1,0:T(8,128)(2,1)S(1)}, u32[]{:S(2)}, u32[]{:S(2)}) collective-permute-start(bf16[512,256]{1,0:T(8,128)(2,1)S(1)} %copy-done.1), channel_id=1, source_target_pairs={{0,64},{32,96},{64,0},{96,32},{1,65},{33,97},{65,1},{97,33},{2,66}... | collective-permute-start | bytes 786440 | tf_op jit(solution)/shard_map/ppermute | solution.py:26
  53.2 26.6 %collective-permute-start.4 = (bf16[512,256]{1,0:T(8,128)(2,1)S(1)}, bf16[512,256]{1,0:T(8,128)(2,1)S(1)}, u32[]{:S(2)}, u32[]{:S(2)}) collective-permute-start(bf16[512,256]{1,0:T(8,128)(2,1)S(1)} %copy-done.1), channel_id=1, source_target_pairs={{0,96},{32,64},{64,32},{96,0},{1,97},{33,65},{65,33},{97,1},{2,98}... | collective-permute-start | bytes 786440 | tf_op jit(solution)/shard_map/ppermute | solution.py:26
  55.4 11.1 %collective-permute-start.10 = (bf16[64,256]{1,0:T(8,128)(2,1)S(1)}, bf16[64,256]{1,0:T(8,128)(2,1)S(1)}, u32[]{:S(2)}, u32[]{:S(2)}) collective-permute-start(bf16[64,256]{1,0:T(8,128)(2,1)S(1)} %copy-done), channel_id=1, source_target_pairs={{0,128},{128,0},{256,384},{384,256},{1,129},{129,1},{257,385},{385... | collective-permute-start | bytes 98312 | tf_op jit(solution)/shard_map/ppermute | solution.py:26
  66.4 11.1 %collective-permute-start.11 = (bf16[128,256]{1,0:T(8,128)(2,1)S(1)}, bf16[128,256]{1,0:T(8,128)(2,1)S(1)}, u32[]{:S(2)}, u32[]{:S(2)}) collective-permute-start(bf16[128,256]{1,0:T(8,128)(2,1)S(1)} %pad_maximum_fusion.4), channel_id=1, source_target_pairs={{0,384},{128,256},{256,128},{384,0},{1,385},{129,257},{257,129},{3... | collective-permute-start | bytes 196616 | tf_op jit(solution)/shard_map/ppermute | solution.py:26
  77.6 52.1 %collective-permute-start.12 = (bf16[256,256]{1,0:T(8,128)(2,1)S(1)}, bf16[256,256]{1,0:T(8,128)(2,1)S(1)}, u32[]{:S(2)}, u32[]{:S(2)}) collective-permute-start(bf16[256,256]{1,0:T(8,128)(2,1)S(1)} %pad_maximum_fusion.1), channel_id=1, source_target_pairs={{0,32},{32,0},{64,96},{96,64},{1,33},{33,1},{65,97},{97,65},{2,34}... | collective-permute-start | bytes 393224 | tf_op jit(solution)/shard_map/ppermute | solution.py:26
  80.4 18.4 %collective-permute-start.5 = (bf16[144,256]{1,0:T(8,128)(2,1)S(1)}, bf16[144,256]{1,0:T(8,128)(2,1)S(1)}, u32[]{:S(2)}, u32[]{:S(2)}) collective-permute-start(bf16[144,256]{1,0:T(8,128)(2,1)S(1)} %get-tuple-element.13), channel_id=1, source_target_pairs={{0,128},{128,0},{256,384},{384,256},{1,129},{129,1},{257,385},{385... | collective-permute-start | bytes 221192 | tf_op jit(solution)/shard_map/ppermute | solution.py:26
  89.6 10.2 %collective-permute-start.6 = (bf16[144,256]{1,0:T(8,128)(2,1)S(1)}, bf16[144,256]{1,0:T(8,128)(2,1)S(1)}, u32[]{:S(2)}, u32[]{:S(2)}) collective-permute-start(bf16[144,256]{1,0:T(8,128)(2,1)S(1)} %get-tuple-element.14), channel_id=1, source_target_pairs={{0,384},{128,256},{256,128},{384,0},{1,385},{129,257},{257,129},{3... | collective-permute-start | bytes 221192 | tf_op jit(solution)/shard_map/ppermute | solution.py:26
  92.4 16.2 %collective-permute-start.7 = (bf16[144,256]{1,0:T(8,128)(2,1)S(1)}, bf16[144,256]{1,0:T(8,128)(2,1)S(1)}, u32[]{:S(2)}, u32[]{:S(2)}) collective-permute-start(bf16[144,256]{1,0:T(8,128)(2,1)S(1)} %get-tuple-element.15), channel_id=1, source_target_pairs={{0,256},{128,384},{256,0},{384,128},{1,257},{129,385},{257,1},{385... | collective-permute-start | bytes 221192 | tf_op jit(solution)/shard_map/ppermute | solution.py:26
  108.7 9.7 %collective-permute-start.14 = (bf16[64,256]{1,0:T(8,128)(2,1)S(1)}, bf16[64,256]{1,0:T(8,128)(2,1)S(1)}, u32[]{:S(2)}, u32[]{:S(2)}) collective-permute-start(bf16[64,256]{1,0:T(8,128)(2,1)S(1)} %shard_map.62), channel_id=1, source_target_pairs={{0,128},{128,0},{256,384},{384,256},{1,129},{129,1},{257,385},{385... | collective-permute-start | bytes 98312 | tf_op jit(solution)/shard_map/ppermute | solution.py:26
  114.1 11.1 %collective-permute-start.8 = (bf16[256,256]{1,0:T(8,128)(2,1)S(1)}, bf16[256,256]{1,0:T(8,128)(2,1)S(1)}, u32[]{:S(2)}, u32[]{:S(2)}) collective-permute-start(bf16[256,256]{1,0:T(8,128)(2,1)S(1)} %pad_maximum_fusion), channel_id=1, source_target_pairs={{0,32},{32,0},{64,96},{96,64},{1,33},{33,1},{65,97},{97,65},{2,34}... | collective-permute-start | bytes 393224 | tf_op jit(solution)/shard_map/ppermute | solution.py:26
  118.5 13.9 %collective-permute-start.15 = (bf16[128,256]{1,0:T(8,128)(2,1)S(1)}, bf16[128,256]{1,0:T(8,128)(2,1)S(1)}, u32[]{:S(2)}, u32[]{:S(2)}) collective-permute-start(bf16[128,256]{1,0:T(8,128)(2,1)S(1)} %pad_maximum_fusion.5), channel_id=1, source_target_pairs={{0,384},{128,256},{256,128},{384,0},{1,385},{129,257},{257,129},{3... | collective-permute-start | bytes 196616 | tf_op jit(solution)/shard_map/ppermute | solution.py:26
  125.3 18.2 %collective-permute-start.9 = (bf16[512,256]{1,0:T(8,128)(2,1)S(1)}, bf16[512,256]{1,0:T(8,128)(2,1)S(1)}, u32[]{:S(2)}, u32[]{:S(2)}) collective-permute-start(bf16[512,256]{1,0:T(8,128)(2,1)S(1)} %constant_dynamic-update-slice_fusion.6.b0), channel_id=1, source_target_pairs={{0,96},{32,64},{64,32},{96,0},{1,97},{33,65},{65,33},{97,1},{2,98}... | collective-permute-start | bytes 786440 | tf_op jit(solution)/shard_map/ppermute | solution.py:26
  129.7 22.1 %collective-permute-start.13 = (bf16[512,256]{1,0:T(8,128)(2,1)S(1)}, bf16[512,256]{1,0:T(8,128)(2,1)S(1)}, u32[]{:S(2)}, u32[]{:S(2)}) collective-permute-start(bf16[512,256]{1,0:T(8,128)(2,1)S(1)} %constant_dynamic-update-slice_fusion.11.t0), channel_id=1, source_target_pairs={{0,96},{32,64},{64,32},{96,0},{1,97},{33,65},{65,33},{97,1},{2,98}... | collective-permute-start | bytes 786440 | tf_op jit(solution)/shard_map/ppermute | solution.py:26
  132.4 21.0 %collective-permute-start.16 = (bf16[256,256]{1,0:T(8,128)(2,1)S(1)}, bf16[256,256]{1,0:T(8,128)(2,1)S(1)}, u32[]{:S(2)}, u32[]{:S(2)}) collective-permute-start(bf16[256,256]{1,0:T(8,128)(2,1)S(1)} %pad_maximum_fusion.2.c0), channel_id=1, source_target_pairs={{0,32},{32,0},{64,96},{96,64},{1,33},{33,1},{65,97},{97,65},{2,34}... | collective-permute-start | bytes 393224 | tf_op jit(solution)/shard_map/ppermute | solution.py:26
  137.0 16.4 %collective-permute-start.17 = (bf16[256,256]{1,0:T(8,128)(2,1)S(1)}, bf16[256,256]{1,0:T(8,128)(2,1)S(1)}, u32[]{:S(2)}, u32[]{:S(2)}) collective-permute-start(bf16[256,256]{1,0:T(8,128)(2,1)S(1)} %pad_maximum_fusion.2.c0), channel_id=1, source_target_pairs={{0,96},{32,64},{64,32},{96,0},{1,97},{33,65},{65,33},{97,1},{2,98}... | collective-permute-start | bytes 393224 | tf_op jit(solution)/shard_map/ppermute | solution.py:26
  141.5 11.9 %collective-permute-start.18 = (bf16[256,256]{1,0:T(8,128)(2,1)S(1)}, bf16[256,256]{1,0:T(8,128)(2,1)S(1)}, u32[]{:S(2)}, u32[]{:S(2)}) collective-permute-start(bf16[256,256]{1,0:T(8,128)(2,1)S(1)} %pad_maximum_fusion.2.c0), channel_id=1, source_target_pairs={{0,64},{32,96},{64,0},{96,32},{1,65},{33,97},{65,1},{97,33},{2,66}... | collective-permute-start | bytes 393224 | tf_op jit(solution)/shard_map/ppermute | solution.py:26

commit v2 on v1

--- a/solution.py
+++ b/solution.py
@@ -30,6 +30,20 @@
     return jnp.concatenate([value, swap(value, axis, bits)], axis=0)
 
 
+def transpose(value):
+    return lax.ppermute(
+        value,
+        AXES,
+        [
+            ((((a * 4 + b) * 4 + d) * 8 + e), (((d * 4 + b) * 4 + a) * 8 + e))
+            for a in range(4)
+            for b in range(4)
+            for d in range(4)
+            for e in range(8)
+        ],
+    )
+
+
 def spread(load, axis):
     parts = jnp.broadcast_to(load[None], (4, *load.shape))
     parts = lax.all_to_all(parts, axis, 0, 0, tiled=True)
@@ -60,8 +74,11 @@
     return lax.dot_general(a, b, (((0,), (0,)), ((), ())), preferred_element_type=F32)
 
 
-def project_kernel(mine, other, gain, p0, p1, p2, p3, keep, s1, s2, s3, acc, sq):
-    zh, y, c = [lax.axis_index(a) for a in ("zh", "y", "c")]
+def project_kernel(mine, other, gain, p0, p1, p2, p3, keep, s1, s2, s3, column, acc, sq):
+    zh, y, x, zl, c = [lax.axis_index(a) for a in AXES]
+    for i, z_rel in enumerate((0, 1, 3, 2)):
+        at = pl.multiple_of(64 + ((x ^ z_rel) * 4 + zl) * 64, 64)
+        column[64 * i : 64 * i + 64, :] = mine[pl.ds(at, 64), :]
     total = jnp.zeros((256, 256), F32)
     squares = jnp.zeros((256, 256), F32)
     for y_rel, proj in enumerate((p0, p1, p2, p3)):
@@ -177,33 +194,21 @@
     band = jnp.where(is_band, tokens, jnp.zeros_like(tokens))
     gains = gain.reshape(32, 256)
 
-    turned = lax.ppermute(
-        tokens,
-        AXES,
-        [
-            ((((a * 4 + b) * 4 + d) * 8 + e), (((d * 4 + b) * 4 + a) * 8 + e))
-            for a in range(4)
-            for b in range(4)
-            for d in range(4)
-            for e in range(8)
-        ],
-    )
+    turned = transpose(tokens)
     weights = [proj] + [swap(proj, "y", k) for k in (1, 2, 3)]
 
     load = jnp.concatenate([band, turned], axis=0)
     load, gains = lax.optimization_barrier((load, gains))
     load, band = spread(load, "zl")
-    load, early = lax.optimization_barrier((load, tokens))
-    blocks = double(early, "zh", 1)
     load, band = spread(load, "x")
-    blocks = double(blocks, "zh", 3)
     other = swap(load, "c", 1, 2)
     band = band + other[:64]
 
     part = jax.ShapeDtypeStruct((144, 256), BF16)
-    keep, s1, s2, s3 = call(
+    block = jax.ShapeDtypeStruct((256, 256), BF16)
+    keep, s1, s2, s3, column = call(
         project_kernel,
-        (jax.ShapeDtypeStruct((80, 256), F32), part, part, part),
+        (jax.ShapeDtypeStruct((80, 256), F32), part, part, part, block),
         load,
         other,
         gains,
@@ -211,7 +216,7 @@
         scratch=(pltpu.VMEM((256, 256), F32), pltpu.VMEM((256, 256), F32)),
     )
     r2, r1, r3 = swap(s2, "zh", 2), swap(s1, "zh", 1), swap(s3, "zh", 3)
-    blocks = double(blocks, "y", 1)
+    blocks = double(transpose(column), "y", 1)
     blocks = [blocks, swap(blocks, "y", 3)]
     bands = jnp.concatenate([band] + [r[80:144] for r in (r1, r3, r2)], axis=0)
     bands = double(bands, "y", 1)

time: 158 us -> 156 us (0.987)
  the two profiles are of different devices: /device:TPU:6 before, /device:TPU:24 now
where the time goes in v2:
time: 156 us; the launch traced here: 155 us
  starting transfers between devices  61.4 us (39%)
  blocking collectives  40.7 us (26%)
  waiting for transfers between devices  37.7 us (24%)
  Pallas kernels  12.2 us (8%)
  between operations  1.72 us (1%)
    ppermute x16, starting transfers between devices, swap(): return lax.ppermute(value, axis, [(i, i ^ bits) for i in range(size)])  59.3 us
    all_to_all x2, blocking collectives, spread(): parts = lax.all_to_all(parts, axis, 0, 0, tiled=True)  40.7 us
    ppermute x16, waiting for transfers between devices, swap(): return lax.ppermute(value, axis, [(i, i ^ bits) for i in range(size)])  37.7 us
    pallas_call x5, Pallas kernels, call(): pl.pallas_call(kernel, out_shape=outs, in_specs=[smem] * n_scalars + [vme...  12.2 us
  transfers between devices with their start and end apart: 18, of which 7 were waited for; matrix products, arithmetic and copies ran while one was open for 0% of the time, Pallas kernels for 6%

profile of v2, /device:TPU:24, one launch (start us, length us, event | category | flops | bytes accessed | tf_op | source)
XLA Modules:
  0.0 154.8 jit_solution(14534798571619169905)
XLA Ops:
  0.6 1.4 collective-permute-start
  2.7 0.0 copy-start.2
  2.7 0.7 copy-done.2
  3.5 0.0 collective-permute-done
  3.5 15.3 %all_to_all.10 = bf16[4,128,256]{2,1,0:T(8,128)(2,1)S(1)} all-to-all(bf16[4,128,256]{2,1,0:T(8,128)(2,1)S(1)} %broadcast_in_dim.7), channel_id=1, replica_groups=mesh['zh'=4,'y'=4,'x'=4,'zl'=4,'c'=2] {'zl'}, dimensions={0} | all-to-all | bytes 524288 | tf_op jit(solution)/shard_map/all_to_all | solution.py:49
  18.9 25.4 %all_to_all.11 = bf16[4,320,256]{2,1,0:T(8,128)(2,1)S(1)} all-to-all(bf16[4,320,256]{2,1,0:T(8,128)(2,1)S(1)} %broadcast_in_dim.8), channel_id=1, replica_groups=mesh['zh'=4,'y'=4,'x'=4,'zl'=4,'c'=2] {'x'}, dimensions={0} | all-to-all | bytes 1310720 | tf_op jit(solution)/shard_map/all_to_all | solution.py:49
  44.4 0.0 copy-start
  44.4 2.1 %collective-permute-start.1 = (bf16[1088,256]{1,0:T(8,128)(2,1)S(1)}, bf16[1088,256]{1,0:T(8,128)(2,1)S(1)}, u32[]{:S(2)}, u32[]{:S(2)}) collective-permute-start(bf16[1088,256]{1,0:T(8,128)(2,1)S(1)} %fusion.mine), channel_id=1, source_target_pairs={{0,1},{1,0},{2,3},{3,2},{4,5},{5,4},{6,7},{7,6},{8,9},{9,8},{10,11... | collective-permute-start | bytes 1671176 | tf_op jit(solution)/shard_map/ppermute | solution.py:26
  46.5 2.7 %collective-permute-start.2 = (bf16[512,256]{1,0:T(8,128)(2,1)S(1)}, bf16[512,256]{1,0:T(8,128)(2,1)S(1)}, u32[]{:S(2)}, u32[]{:S(2)}) collective-permute-start(bf16[512,256]{1,0:T(8,128)(2,1)S(1)} %copy-done), channel_id=1, source_target_pairs={{0,32},{32,0},{64,96},{96,64},{1,33},{33,1},{65,97},{97,65},{2,34}... | collective-permute-start | bytes 786440 | tf_op jit(solution)/shard_map/ppermute | solution.py:26
  49.2 2.8 %collective-permute-start.3 = (bf16[512,256]{1,0:T(8,128)(2,1)S(1)}, bf16[512,256]{1,0:T(8,128)(2,1)S(1)}, u32[]{:S(2)}, u32[]{:S(2)}) collective-permute-start(bf16[512,256]{1,0:T(8,128)(2,1)S(1)} %copy-done), channel_id=1, source_target_pairs={{0,64},{32,96},{64,0},{96,32},{1,65},{33,97},{65,1},{97,33},{2,66}... | collective-permute-start | bytes 786440 | tf_op jit(solution)/shard_map/ppermute | solution.py:26
  52.0 4.9 %collective-permute-start.4 = (bf16[512,256]{1,0:T(8,128)(2,1)S(1)}, bf16[512,256]{1,0:T(8,128)(2,1)S(1)}, u32[]{:S(2)}, u32[]{:S(2)}) collective-permute-start(bf16[512,256]{1,0:T(8,128)(2,1)S(1)} %copy-done), channel_id=1, source_target_pairs={{0,96},{32,64},{64,32},{96,0},{1,97},{33,65},{65,33},{97,1},{2,98}... | collective-permute-start | bytes 786440 | tf_op jit(solution)/shard_map/ppermute | solution.py:26
  57.0 0.6 collective-permute-done.2.p1
  57.6 4.9 %collective-permute-done.3.p2 = bf16[512,256]{1,0:T(8,128)(2,1)S(1)} collective-permute-done((bf16[512,256]{1,0:T(8,128)(2,1)S(1)}, bf16[512,256]{1,0:T(8,128)(2,1)S(1)}, u32[]{:S(2)}, u32[]{:S(2)}) %collective-permute-start.3) | collective-permute-done | bytes 262176 | tf_op jit(solution)/shard_map/ppermute | solution.py:26
  62.5 5.5 %collective-permute-done.4.p3 = bf16[512,256]{1,0:T(8,128)(2,1)S(1)} collective-permute-done((bf16[512,256]{1,0:T(8,128)(2,1)S(1)}, bf16[512,256]{1,0:T(8,128)(2,1)S(1)}, u32[]{:S(2)}, u32[]{:S(2)}) %collective-permute-start.4) | collective-permute-done | bytes 262176 | tf_op jit(solution)/shard_map/ppermute | solution.py:26
  68.0 0.0 collective-permute-done.1.other
  68.0 0.6 shard_map.59
  68.6 8.8 %collective-permute-start.5 = (bf16[144,256]{1,0:T(8,128)(2,1)S(1)}, bf16[144,256]{1,0:T(8,128)(2,1)S(1)}, u32[]{:S(2)}, u32[]{:S(2)}) collective-permute-start(bf16[144,256]{1,0:T(8,128)(2,1)S(1)} %get-tuple-element.11), channel_id=1, source_target_pairs={{0,128},{128,0},{256,384},{384,256},{1,129},{129,1},{257,385},{385... | collective-permute-start | bytes 221192 | tf_op jit(solution)/shard_map/ppermute | solution.py:26
  77.4 5.0 %collective-permute-start.6 = (bf16[144,256]{1,0:T(8,128)(2,1)S(1)}, bf16[144,256]{1,0:T(8,128)(2,1)S(1)}, u32[]{:S(2)}, u32[]{:S(2)}) collective-permute-start(bf16[144,256]{1,0:T(8,128)(2,1)S(1)} %get-tuple-element.12), channel_id=1, source_target_pairs={{0,384},{128,256},{256,128},{384,0},{1,385},{129,257},{257,129},{3... | collective-permute-start | bytes 221192 | tf_op jit(solution)/shard_map/ppermute | solution.py:26
  82.4 4.2 %collective-permute-start.7 = (bf16[144,256]{1,0:T(8,128)(2,1)S(1)}, bf16[144,256]{1,0:T(8,128)(2,1)S(1)}, u32[]{:S(2)}, u32[]{:S(2)}) collective-permute-start(bf16[144,256]{1,0:T(8,128)(2,1)S(1)} %get-tuple-element.13), channel_id=1, source_target_pairs={{0,256},{128,384},{256,0},{384,128},{1,257},{129,385},{257,1},{385... | collective-permute-start | bytes 221192 | tf_op jit(solution)/shard_map/ppermute | solution.py:26
  86.6 0.7 collective-permute-start.10
  87.3 0.0 copy-start.1
  87.3 0.0 collective-permute-done.5.r1
  87.3 5.3 %collective-permute-done.6.r3 = bf16[144,256]{1,0:T(8,128)(2,1)S(1)} collective-permute-done((bf16[144,256]{1,0:T(8,128)(2,1)S(1)}, bf16[144,256]{1,0:T(8,128)(2,1)S(1)}, u32[]{:S(2)}, u32[]{:S(2)}) %collective-permute-start.6) | collective-permute-done | bytes 73760 | tf_op jit(solution)/shard_map/ppermute | solution.py:26
  92.7 6.6 %collective-permute-done.7.r2 = bf16[144,256]{1,0:T(8,128)(2,1)S(1)} collective-permute-done((bf16[144,256]{1,0:T(8,128)(2,1)S(1)}, bf16[144,256]{1,0:T(8,128)(2,1)S(1)}, u32[]{:S(2)}, u32[]{:S(2)}) %collective-permute-start.7) | collective-permute-done | bytes 73760 | tf_op jit(solution)/shard_map/ppermute | solution.py:26
  99.2 0.0 copy-done.1
  99.2 0.1 shard_map.62
  99.3 3.2 %collective-permute-start.13 = (bf16[64,256]{1,0:T(8,128)(2,1)S(1)}, bf16[64,256]{1,0:T(8,128)(2,1)S(1)}, u32[]{:S(2)}, u32[]{:S(2)}) collective-permute-start(bf16[64,256]{1,0:T(8,128)(2,1)S(1)} %shard_map.62), channel_id=1, source_target_pairs={{0,128},{128,0},{256,384},{384,256},{1,129},{129,1},{257,385},{385... | collective-permute-start | bytes 98312 | tf_op jit(solution)/shard_map/ppermute | solution.py:26
  102.6 2.2 %collective-permute-start.8 = (bf16[256,256]{1,0:T(8,128)(2,1)S(1)}, bf16[256,256]{1,0:T(8,128)(2,1)S(1)}, u32[]{:S(2)}, u32[]{:S(2)}) collective-permute-start(bf16[256,256]{1,0:T(8,128)(2,1)S(1)} %pad_maximum_fusion), channel_id=1, source_target_pairs={{0,32},{32,0},{64,96},{96,64},{1,33},{33,1},{65,97},{97,65},{2,34}... | collective-permute-start | bytes 393224 | tf_op jit(solution)/shard_map/ppermute | solution.py:26
  104.8 14.6 %collective-permute-done.13 = bf16[64,256]{1,0:T(8,128)(2,1)S(1)} collective-permute-done((bf16[64,256]{1,0:T(8,128)(2,1)S(1)}, bf16[64,256]{1,0:T(8,128)(2,1)S(1)}, u32[]{:S(2)}, u32[]{:S(2)}) %collective-permute-start.13) | collective-permute-done | bytes 32800 | tf_op jit(solution)/shard_map/ppermute | solution.py:26
  119.4 1.9 %collective-permute-start.14 = (bf16[128,256]{1,0:T(8,128)(2,1)S(1)}, bf16[128,256]{1,0:T(8,128)(2,1)S(1)}, u32[]{:S(2)}, u32[]{:S(2)}) collective-permute-start(bf16[128,256]{1,0:T(8,128)(2,1)S(1)} %pad_maximum_fusion.3), channel_id=1, source_target_pairs={{0,384},{128,256},{256,128},{384,0},{1,385},{129,257},{257,129},{3... | collective-permute-start | bytes 196616 | tf_op jit(solution)/shard_map/ppermute | solution.py:26
  121.3 0.0 collective-permute-done.10
  121.3 2.5 %collective-permute-start.11 = (bf16[256,256]{1,0:T(8,128)(2,1)S(1)}, bf16[256,256]{1,0:T(8,128)(2,1)S(1)}, u32[]{:S(2)}, u32[]{:S(2)}) collective-permute-start(bf16[256,256]{1,0:T(8,128)(2,1)S(1)} %collective-permute-done.10), channel_id=1, source_target_pairs={{0,32},{32,0},{64,96},{96,64},{1,33},{33,1},{65,97},{97,65},{2,34}... | collective-permute-start | bytes 393224 | tf_op jit(solution)/shard_map/ppermute | solution.py:26
  123.8 0.0 collective-permute-done.8
  123.9 4.3 %collective-permute-start.9 = (bf16[512,256]{1,0:T(8,128)(2,1)S(1)}, bf16[512,256]{1,0:T(8,128)(2,1)S(1)}, u32[]{:S(2)}, u32[]{:S(2)}) collective-permute-start(bf16[512,256]{1,0:T(8,128)(2,1)S(1)} %constant_dynamic-update-slice_fusion.6.b0), channel_id=1, source_target_pairs={{0,96},{32,64},{64,32},{96,0},{1,97},{33,65},{65,33},{97,1},{2,98}... | collective-permute-start | bytes 786440 | tf_op jit(solution)/shard_map/ppermute | solution.py:26
  128.2 0.2 collective-permute-done.11
  128.4 4.9 %collective-permute-start.12 = (bf16[512,256]{1,0:T(8,128)(2,1)S(1)}, bf16[512,256]{1,0:T(8,128)(2,1)S(1)}, u32[]{:S(2)}, u32[]{:S(2)}) collective-permute-start(bf16[512,256]{1,0:T(8,128)(2,1)S(1)} %constant_dynamic-update-slice_fusion.11.t0), channel_id=1, source_target_pairs={{0,96},{32,64},{64,32},{96,0},{1,97},{33,65},{65,33},{97,1},{2,98}... | collective-permute-start | bytes 786440 | tf_op jit(solution)/shard_map/ppermute | solution.py:26
  133.3 0.0 collective-permute-done.14
  133.4 1.9 %collective-permute-start.15 = (bf16[256,256]{1,0:T(8,128)(2,1)S(1)}, bf16[256,256]{1,0:T(8,128)(2,1)S(1)}, u32[]{:S(2)}, u32[]{:S(2)}) collective-permute-start(bf16[256,256]{1,0:T(8,128)(2,1)S(1)} %pad_maximum_fusion.1.c0), channel_id=1, source_target_pairs={{0,32},{32,0},{64,96},{96,64},{1,33},{33,1},{65,97},{97,65},{2,34}... | collective-permute-start | bytes 393224 | tf_op jit(solution)/shard_map/ppermute | solution.py:26
  135.3 2.8 %collective-permute-start.16 = (bf16[256,256]{1,0:T(8,128)(2,1)S(1)}, bf16[256,256]{1,0:T(8,128)(2,1)S(1)}, u32[]{:S(2)}, u32[]{:S(2)}) collective-permute-start(bf16[256,256]{1,0:T(8,128)(2,1)S(1)} %pad_maximum_fusion.1.c0), channel_id=1, source_target_pairs={{0,96},{32,64},{64,32},{96,0},{1,97},{33,65},{65,33},{97,1},{2,98}... | collective-permute-start | bytes 393224 | tf_op jit(solution)/shard_map/ppermute | solution.py:26
  138.1 5.1 %collective-permute-start.17 = (bf16[256,256]{1,0:T(8,128)(2,1)S(1)}, bf16[256,256]{1,0:T(8,128)(2,1)S(1)}, u32[]{:S(2)}, u32[]{:S(2)}) collective-permute-start(bf16[256,256]{1,0:T(8,128)(2,1)S(1)} %pad_maximum_fusion.1.c0), channel_id=1, source_target_pairs={{0,64},{32,96},{64,0},{96,32},{1,65},{33,97},{65,1},{97,33},{2,66}... | collective-permute-start | bytes 393224 | tf_op jit(solution)/shard_map/ppermute | solution.py:26
  143.2 0.0 collective-permute-done.9.b1
  143.2 8.3 %shard_map.60.inverse = f32[256,256]{1,0:T(8,128)S(1)} custom-call(bf16[512,256]{1,0:T(8,128)(2,1)S(1)} %constant_dynamic-update-slice_fusion.6.b0, bf16[512,256]{1,0:T(8,128)(2,1)S(1)} %collective-permute-done.9.b1), custom_call_target="tpu_custom_call" | custom-call | tf_op jit(solution)/shard_map/pallas_call | solution.py:64
  151.5 0.0 collective-permute-done.15.c1
  151.6 0.0 collective-permute-done.16.c2
  151.6 0.0 collective-permute-done.17.c3
  151.6 1.6 %shard_map.63 = f32[256,256]{1,0:T(8,128)} custom-call(bf16[512,256]{1,0:T(8,128)(2,1)S(1)} %constant_dynamic-update-slice_fusion.6.b0, bf16[512,256]{1,0:T(8,128)(2,1)S(1)} %collective-permute-done.9.b1, bf16[256,256]{1,0:T(8,128)(2,1)S(1)} %pad_maximum_fusion.1.c0, bf16[256,256]{1,0:T(8,128)(2,1)S(1)} %collective-permute-done.15.c1, ...), custom_call_target="tpu_custom_call" | custom-call | tf_op jit(solution)/shard_map/pallas_call | solution.py:64
  153.2 0.0 collective-permute-done.12.t1
  153.2 1.6 %shard_map.61 = f32[256,256]{1,0:T(8,128)} custom-call(s32[1]{0:T(128)} %bitcast.1.is_band, bf16[512,256]{1,0:T(8,128)(2,1)S(1)} %constant_dynamic-update-slice_fusion.6.b0, bf16[512,256]{1,0:T(8,128)(2,1)S(1)} %collective-permute-done.9.b1, bf16[512,256]{1,0:T(8,128)(2,1)S(1)} %constant_dynamic-update-slice_fusion.11.t0, ...), custom_call_target="tpu_custom_call" | custom-call | tf_op jit(solution)/shard_map/pallas_call | solution.py:64
  (26 shorter events, 0.3 us)
Async XLA Ops:
  0.6 2.8 %collective-permute-start = (bf16[64,256]{1,0:T(8,128)(2,1)}, bf16[64,256]{1,0:T(8,128)(2,1)S(1)}, u32[]{:S(2)}, u32[]{:S(2)}) collective-permute-start(bf16[64,256]{1,0:T(8,128)(2,1)} %tokens.1), channel_id=1, source_target_pairs={{0,0},{1,1},{2,2},{3,3},{4,4},{5,5},{6,6},{7,7},{8,128},{9,129},{1... | collective-permute-start | bytes 98312 | tf_op jit(solution)/shard_map/ppermute | solution.py:34
  2.7 0.8 copy-start.2
  44.4 2.1 %copy-start = (bf16[512,256]{1,0:T(8,128)(2,1)S(1)}, bf16[512,256]{1,0:T(8,128)(2,1)}, u32[]{:S(2)}) copy-start(bf16[512,256]{1,0:T(8,128)(2,1)} %p0.1) | copy-start | bytes 786436
  44.4 23.6 %collective-permute-start.1 = (bf16[1088,256]{1,0:T(8,128)(2,1)S(1)}, bf16[1088,256]{1,0:T(8,128)(2,1)S(1)}, u32[]{:S(2)}, u32[]{:S(2)}) collective-permute-start(bf16[1088,256]{1,0:T(8,128)(2,1)S(1)} %fusion.mine), channel_id=1, source_target_pairs={{0,1},{1,0},{2,3},{3,2},{4,5},{5,4},{6,7},{7,6},{8,9},{9,8},{10,11... | collective-permute-start | bytes 1671176 | tf_op jit(solution)/shard_map/ppermute | solution.py:26
  46.5 11.1 %collective-permute-start.2 = (bf16[512,256]{1,0:T(8,128)(2,1)S(1)}, bf16[512,256]{1,0:T(8,128)(2,1)S(1)}, u32[]{:S(2)}, u32[]{:S(2)}) collective-permute-start(bf16[512,256]{1,0:T(8,128)(2,1)S(1)} %copy-done), channel_id=1, source_target_pairs={{0,32},{32,0},{64,96},{96,64},{1,33},{33,1},{65,97},{97,65},{2,34}... | collective-permute-start | bytes 786440 | tf_op jit(solution)/shard_map/ppermute | solution.py:26
  49.2 13.3 %collective-permute-start.3 = (bf16[512,256]{1,0:T(8,128)(2,1)S(1)}, bf16[512,256]{1,0:T(8,128)(2,1)S(1)}, u32[]{:S(2)}, u32[]{:S(2)}) collective-permute-start(bf16[512,256]{1,0:T(8,128)(2,1)S(1)} %copy-done), channel_id=1, source_target_pairs={{0,64},{32,96},{64,0},{96,32},{1,65},{33,97},{65,1},{97,33},{2,66}... | collective-permute-start | bytes 786440 | tf_op jit(solution)/shard_map/ppermute | solution.py:26
  52.0 16.0 %collective-permute-start.4 = (bf16[512,256]{1,0:T(8,128)(2,1)S(1)}, bf16[512,256]{1,0:T(8,128)(2,1)S(1)}, u32[]{:S(2)}, u32[]{:S(2)}) collective-permute-start(bf16[512,256]{1,0:T(8,128)(2,1)S(1)} %copy-done), channel_id=1, source_target_pairs={{0,96},{32,64},{64,32},{96,0},{1,97},{33,65},{65,33},{97,1},{2,98}... | collective-permute-start | bytes 786440 | tf_op jit(solution)/shard_map/ppermute | solution.py:26
  68.6 18.8 %collective-permute-start.5 = (bf16[144,256]{1,0:T(8,128)(2,1)S(1)}, bf16[144,256]{1,0:T(8,128)(2,1)S(1)}, u32[]{:S(2)}, u32[]{:S(2)}) collective-permute-start(bf16[144,256]{1,0:T(8,128)(2,1)S(1)} %get-tuple-element.11), channel_id=1, source_target_pairs={{0,128},{128,0},{256,384},{384,256},{1,129},{129,1},{257,385},{385... | collective-permute-start | bytes 221192 | tf_op jit(solution)/shard_map/ppermute | solution.py:26
  77.4 15.3 %collective-permute-start.6 = (bf16[144,256]{1,0:T(8,128)(2,1)S(1)}, bf16[144,256]{1,0:T(8,128)(2,1)S(1)}, u32[]{:S(2)}, u32[]{:S(2)}) collective-permute-start(bf16[144,256]{1,0:T(8,128)(2,1)S(1)} %get-tuple-element.12), channel_id=1, source_target_pairs={{0,384},{128,256},{256,128},{384,0},{1,385},{129,257},{257,129},{3... | collective-permute-start | bytes 221192 | tf_op jit(solution)/shard_map/ppermute | solution.py:26
  82.4 16.8 %collective-permute-start.7 = (bf16[144,256]{1,0:T(8,128)(2,1)S(1)}, bf16[144,256]{1,0:T(8,128)(2,1)S(1)}, u32[]{:S(2)}, u32[]{:S(2)}) collective-permute-start(bf16[144,256]{1,0:T(8,128)(2,1)S(1)} %get-tuple-element.13), channel_id=1, source_target_pairs={{0,256},{128,384},{256,0},{384,128},{1,257},{129,385},{257,1},{385... | collective-permute-start | bytes 221192 | tf_op jit(solution)/shard_map/ppermute | solution.py:26
  86.6 34.7 %collective-permute-start.10 = (bf16[256,256]{1,0:T(8,128)(2,1)S(1)}, bf16[256,256]{1,0:T(8,128)(2,1)S(1)}, u32[]{:S(2)}, u32[]{:S(2)}) collective-permute-start(bf16[256,256]{1,0:T(8,128)(2,1)S(1)} %get-tuple-element.14), channel_id=1, source_target_pairs={{0,0},{1,1},{2,2},{3,3},{4,4},{5,5},{6,6},{7,7},{8,128},{9,129},{1... | collective-permute-start | bytes 393224 | tf_op jit(solution)/shard_map/ppermute | solution.py:34
  87.3 11.9 %copy-start.1 = (bf16[64,256]{1,0:T(8,128)(2,1)S(1)}, bf16[64,256]{1,0:T(8,128)(2,1)}, u32[]{:S(2)}) copy-start(bf16[64,256]{1,0:T(8,128)(2,1)} %tokens.1) | copy-start | bytes 98308
  99.3 20.0 %collective-permute-start.13 = (bf16[64,256]{1,0:T(8,128)(2,1)S(1)}, bf16[64,256]{1,0:T(8,128)(2,1)S(1)}, u32[]{:S(2)}, u32[]{:S(2)}) collective-permute-start(bf16[64,256]{1,0:T(8,128)(2,1)S(1)} %shard_map.62), channel_id=1, source_target_pairs={{0,128},{128,0},{256,384},{384,256},{1,129},{129,1},{257,385},{385... | collective-permute-start | bytes 98312 | tf_op jit(solution)/shard_map/ppermute | solution.py:26
  102.6 21.3 %collective-permute-start.8 = (bf16[256,256]{1,0:T(8,128)(2,1)S(1)}, bf16[256,256]{1,0:T(8,128)(2,1)S(1)}, u32[]{:S(2)}, u32[]{:S(2)}) collective-permute-start(bf16[256,256]{1,0:T(8,128)(2,1)S(1)} %pad_maximum_fusion), channel_id=1, source_target_pairs={{0,32},{32,0},{64,96},{96,64},{1,33},{33,1},{65,97},{97,65},{2,34}... | collective-permute-start | bytes 393224 | tf_op jit(solution)/shard_map/ppermute | solution.py:26
  119.4 13.9 %collective-permute-start.14 = (bf16[128,256]{1,0:T(8,128)(2,1)S(1)}, bf16[128,256]{1,0:T(8,128)(2,1)S(1)}, u32[]{:S(2)}, u32[]{:S(2)}) collective-permute-start(bf16[128,256]{1,0:T(8,128)(2,1)S(1)} %pad_maximum_fusion.3), channel_id=1, source_target_pairs={{0,384},{128,256},{256,128},{384,0},{1,385},{129,257},{257,129},{3... | collective-permute-start | bytes 196616 | tf_op jit(solution)/shard_map/ppermute | solution.py:26
  121.3 7.1 %collective-permute-start.11 = (bf16[256,256]{1,0:T(8,128)(2,1)S(1)}, bf16[256,256]{1,0:T(8,128)(2,1)S(1)}, u32[]{:S(2)}, u32[]{:S(2)}) collective-permute-start(bf16[256,256]{1,0:T(8,128)(2,1)S(1)} %collective-permute-done.10), channel_id=1, source_target_pairs={{0,32},{32,0},{64,96},{96,64},{1,33},{33,1},{65,97},{97,65},{2,34}... | collective-permute-start | bytes 393224 | tf_op jit(solution)/shard_map/ppermute | solution.py:26
  123.9 19.3 %collective-permute-start.9 = (bf16[512,256]{1,0:T(8,128)(2,1)S(1)}, bf16[512,256]{1,0:T(8,128)(2,1)S(1)}, u32[]{:S(2)}, u32[]{:S(2)}) collective-permute-start(bf16[512,256]{1,0:T(8,128)(2,1)S(1)} %constant_dynamic-update-slice_fusion.6.b0), channel_id=1, source_target_pairs={{0,96},{32,64},{64,32},{96,0},{1,97},{33,65},{65,33},{97,1},{2,98}... | collective-permute-start | bytes 786440 | tf_op jit(solution)/shard_map/ppermute | solution.py:26
  128.4 24.8 %collective-permute-start.12 = (bf16[512,256]{1,0:T(8,128)(2,1)S(1)}, bf16[512,256]{1,0:T(8,128)(2,1)S(1)}, u32[]{:S(2)}, u32[]{:S(2)}) collective-permute-start(bf16[512,256]{1,0:T(8,128)(2,1)S(1)} %constant_dynamic-update-slice_fusion.11.t0), channel_id=1, source_target_pairs={{0,96},{32,64},{64,32},{96,0},{1,97},{33,65},{65,33},{97,1},{2,98}... | collective-permute-start | bytes 786440 | tf_op jit(solution)/shard_map/ppermute | solution.py:26
  133.4 18.2 %collective-permute-start.15 = (bf16[256,256]{1,0:T(8,128)(2,1)S(1)}, bf16[256,256]{1,0:T(8,128)(2,1)S(1)}, u32[]{:S(2)}, u32[]{:S(2)}) collective-permute-start(bf16[256,256]{1,0:T(8,128)(2,1)S(1)} %pad_maximum_fusion.1.c0), channel_id=1, source_target_pairs={{0,32},{32,0},{64,96},{96,64},{1,33},{33,1},{65,97},{97,65},{2,34}... | collective-permute-start | bytes 393224 | tf_op jit(solution)/shard_map/ppermute | solution.py:26
  135.3 16.3 %collective-permute-start.16 = (bf16[256,256]{1,0:T(8,128)(2,1)S(1)}, bf16[256,256]{1,0:T(8,128)(2,1)S(1)}, u32[]{:S(2)}, u32[]{:S(2)}) collective-permute-start(bf16[256,256]{1,0:T(8,128)(2,1)S(1)} %pad_maximum_fusion.1.c0), channel_id=1, source_target_pairs={{0,96},{32,64},{64,32},{96,0},{1,97},{33,65},{65,33},{97,1},{2,98}... | collective-permute-start | bytes 393224 | tf_op jit(solution)/shard_map/ppermute | solution.py:26
  138.1 13.5 %collective-permute-start.17 = (bf16[256,256]{1,0:T(8,128)(2,1)S(1)}, bf16[256,256]{1,0:T(8,128)(2,1)S(1)}, u32[]{:S(2)}, u32[]{:S(2)}) collective-permute-start(bf16[256,256]{1,0:T(8,128)(2,1)S(1)} %pad_maximum_fusion.1.c0), channel_id=1, source_target_pairs={{0,64},{32,96},{64,0},{96,32},{1,65},{33,97},{65,1},{97,33},{2,66}... | collective-permute-start | bytes 393224 | tf_op jit(solution)/shard_map/ppermute | solution.py:26

commit v3 on v2

--- a/solution.py
+++ b/solution.py
@@ -174,18 +174,17 @@
             inverse[hi:, :] = inverse[hi:, :] - dot_hi(below, top)
 
 
-def gram_kernel(is_band, b0, b1, t0, t1, inverse, out):
-    total = dot_tn(b0[...], t0[...]) + dot_tn(b1[...], t1[...])
+def solve_kernel(is_band, near, far, both, inverse, panel_rows, solved_cross):
+    y = lax.axis_index("y")
+    total = dot_tn(near[0:256, :], both[y])
+    total = total + dot_tn(near[256:512, :], both[y ^ 1])
+    total = total + dot_tn(far[0:256, :], both[y ^ 3])
+    total = total + dot_tn(far[256:512, :], both[y ^ 2])
     row = lax.broadcasted_iota(jnp.int32, (PANEL, PANEL), 0)
     lane = lax.broadcasted_iota(jnp.int32, (PANEL, PANEL), 1)
     ridge = jnp.where((row == lane) & (is_band[0] == 1), 0.1, 0.0)
-    out[...] = dot_hi(inverse[...], total / TOKENS + ridge)
-
-
-def cross_kernel(b0, b1, c0, c1, c2, c3, inverse, out):
-    total = dot_tn(b0[0:256, :], c0[...]) + dot_tn(b0[256:512, :], c1[...])
-    total = total + dot_tn(b1[0:256, :], c2[...]) + dot_tn(b1[256:512, :], c3[...])
-    out[...] = dot_hi(inverse[...], total * (math.sqrt(D) / TOKENS))
+    panel_rows[...] = dot_hi(inverse[...], total[:, 256:512] / TOKENS + ridge)
+    solved_cross[...] = dot_hi(inverse[...], total[:, 0:256] * (math.sqrt(D) / TOKENS))
 
 
 def steps(tokens, gain, proj, panel_index):
@@ -216,8 +215,7 @@
         scratch=(pltpu.VMEM((256, 256), F32), pltpu.VMEM((256, 256), F32)),
     )
     r2, r1, r3 = swap(s2, "zh", 2), swap(s1, "zh", 1), swap(s3, "zh", 3)
-    blocks = double(transpose(column), "y", 1)
-    blocks = [blocks, swap(blocks, "y", 3)]
+    column = transpose(column)
     bands = jnp.concatenate([band] + [r[80:144] for r in (r1, r3, r2)], axis=0)
     bands = double(bands, "y", 1)
     bands = [bands, swap(bands, "y", 3)]
@@ -225,13 +223,16 @@
     change = call(change_kernel, jax.ShapeDtypeStruct((64, 256), BF16), tokens, keep, r1, r2, r3)
     change = double(change, "zh", 1)
     change = double(change, "zh", 3)
-    changes = [change] + [swap(change, "y", k) for k in (1, 3, 2)]
+    both = jnp.concatenate([change, column], axis=1)
+    both = jnp.broadcast_to(both[None], (4, *both.shape))
+    both = lax.all_to_all(both, "y", 0, 0, tiled=True)
 
     square = jax.ShapeDtypeStruct((PANEL, PANEL), F32)
     inverse = call(factor_kernel, square, *bands, scratch=(pltpu.VMEM((PANEL, PANEL), F32),))
     flag = is_band.astype(jnp.int32).reshape(1)
-    panel_rows = call(gram_kernel, square, flag, *bands, *blocks, inverse, n_scalars=1, final=True)
-    solved_cross = call(cross_kernel, square, *bands, *changes, inverse, final=True)
+    panel_rows, solved_cross = call(
+        solve_kernel, (square, square), flag, *bands, both, inverse, n_scalars=1, final=True
+    )
     return (panel_rows, solved_cross)
 
 

time: 156 us -> 172 us (1.10)
  the two profiles are of different devices: /device:TPU:24 before, /device:TPU:32 now
where the time goes in v3:
time: 172 us; the launch traced here: 171 us
  waiting for transfers between devices  69.8 us (41%)
  starting transfers between devices  47.7 us (28%)
  blocking collectives  39.2 us (23%)
  Pallas kernels  10.8 us (6%)
  local copies, waits for them, and re-layouts  1.98 us (1%)
    ppermute x11, waiting for transfers between devices, swap(): return lax.ppermute(value, axis, [(i, i ^ bits) for i in range(size)])  69.8 us
    ppermute x11, starting transfers between devices, swap(): return lax.ppermute(value, axis, [(i, i ^ bits) for i in range(size)])  42.1 us
    all_to_all x2, blocking collectives, spread(): parts = lax.all_to_all(parts, axis, 0, 0, tiled=True)  39.2 us
    pallas_call x4, Pallas kernels, call(): pl.pallas_call(kernel, out_shape=outs, in_specs=[smem] * n_scalars + [vme...  10.8 us
    all_to_all x1, starting transfers between devices, steps(): both = lax.all_to_all(both, 'y', 0, 0, tiled=True)  3.51 us
  transfers between devices with their start and end apart: 14, of which 9 were waited for; matrix products, arithmetic and copies ran while one was open for 0% of the time, Pallas kernels for 5%

profile of v3, /device:TPU:32, one launch (start us, length us, event | category | flops | bytes accessed | tf_op | source)
XLA Modules:
  0.0 171.3 jit_solution(5378040066953623454)
XLA Ops:
  0.6 1.4 collective-permute-start
  2.7 0.0 copy-start.2
  2.7 0.7 copy-done.2
  3.5 0.0 collective-permute-done
  3.5 14.8 %all_to_all.15 = bf16[4,128,256]{2,1,0:T(8,128)(2,1)S(1)} all-to-all(bf16[4,128,256]{2,1,0:T(8,128)(2,1)S(1)} %broadcast_in_dim.9), channel_id=1, replica_groups=mesh['zh'=4,'y'=4,'x'=4,'zl'=4,'c'=2] {'zl'}, dimensions={0} | all-to-all | bytes 524288 | tf_op jit(solution)/shard_map/all_to_all | solution.py:49
  18.4 24.4 %all_to_all.16 = bf16[4,320,256]{2,1,0:T(8,128)(2,1)S(1)} all-to-all(bf16[4,320,256]{2,1,0:T(8,128)(2,1)S(1)} %broadcast_in_dim.10), channel_id=1, replica_groups=mesh['zh'=4,'y'=4,'x'=4,'zl'=4,'c'=2] {'x'}, dimensions={0} | all-to-all | bytes 1310720 | tf_op jit(solution)/shard_map/all_to_all | solution.py:49
  42.9 0.0 copy-start
  42.9 2.1 %collective-permute-start.1 = (bf16[1088,256]{1,0:T(8,128)(2,1)S(1)}, bf16[1088,256]{1,0:T(8,128)(2,1)S(1)}, u32[]{:S(2)}, u32[]{:S(2)}) collective-permute-start(bf16[1088,256]{1,0:T(8,128)(2,1)S(1)} %fusion.mine), channel_id=1, source_target_pairs={{0,1},{1,0},{2,3},{3,2},{4,5},{5,4},{6,7},{7,6},{8,9},{9,8},{10,11... | collective-permute-start | bytes 1671176 | tf_op jit(solution)/shard_map/ppermute | solution.py:26
  45.0 0.0 copy-done
  45.0 3.5 %collective-permute-start.2 = (bf16[512,256]{1,0:T(8,128)(2,1)S(1)}, bf16[512,256]{1,0:T(8,128)(2,1)S(1)}, u32[]{:S(2)}, u32[]{:S(2)}) collective-permute-start(bf16[512,256]{1,0:T(8,128)(2,1)S(1)} %copy-done), channel_id=1, source_target_pairs={{0,32},{32,0},{64,96},{96,64},{1,33},{33,1},{65,97},{97,65},{2,34}... | collective-permute-start | bytes 786440 | tf_op jit(solution)/shard_map/ppermute | solution.py:26
  48.5 4.8 %collective-permute-start.3 = (bf16[512,256]{1,0:T(8,128)(2,1)S(1)}, bf16[512,256]{1,0:T(8,128)(2,1)S(1)}, u32[]{:S(2)}, u32[]{:S(2)}) collective-permute-start(bf16[512,256]{1,0:T(8,128)(2,1)S(1)} %copy-done), channel_id=1, source_target_pairs={{0,64},{32,96},{64,0},{96,32},{1,65},{33,97},{65,1},{97,33},{2,66}... | collective-permute-start | bytes 786440 | tf_op jit(solution)/shard_map/ppermute | solution.py:26
  53.3 2.1 %collective-permute-start.4 = (bf16[512,256]{1,0:T(8,128)(2,1)S(1)}, bf16[512,256]{1,0:T(8,128)(2,1)S(1)}, u32[]{:S(2)}, u32[]{:S(2)}) collective-permute-start(bf16[512,256]{1,0:T(8,128)(2,1)S(1)} %copy-done), channel_id=1, source_target_pairs={{0,96},{32,64},{64,32},{96,0},{1,97},{33,65},{65,33},{97,1},{2,98}... | collective-permute-start | bytes 786440 | tf_op jit(solution)/shard_map/ppermute | solution.py:26
  55.4 0.6 collective-permute-done.2.p1
  56.1 7.7 %collective-permute-done.3.p2 = bf16[512,256]{1,0:T(8,128)(2,1)S(1)} collective-permute-done((bf16[512,256]{1,0:T(8,128)(2,1)S(1)}, bf16[512,256]{1,0:T(8,128)(2,1)S(1)}, u32[]{:S(2)}, u32[]{:S(2)}) %collective-permute-start.3) | collective-permute-done | bytes 262176 | tf_op jit(solution)/shard_map/ppermute | solution.py:26
  63.8 5.5 %collective-permute-done.4.p3 = bf16[512,256]{1,0:T(8,128)(2,1)S(1)} collective-permute-done((bf16[512,256]{1,0:T(8,128)(2,1)S(1)}, bf16[512,256]{1,0:T(8,128)(2,1)S(1)}, u32[]{:S(2)}, u32[]{:S(2)}) %collective-permute-start.4) | collective-permute-done | bytes 262176 | tf_op jit(solution)/shard_map/ppermute | solution.py:26
  69.3 0.0 collective-permute-done.1.other
  69.3 0.6 shard_map.59
  69.9 11.3 %collective-permute-start.7 = (bf16[144,256]{1,0:T(8,128)(2,1)S(1)}, bf16[144,256]{1,0:T(8,128)(2,1)S(1)}, u32[]{:S(2)}, u32[]{:S(2)}) collective-permute-start(bf16[144,256]{1,0:T(8,128)(2,1)S(1)} %get-tuple-element.13), channel_id=1, source_target_pairs={{0,256},{128,384},{256,0},{384,128},{1,257},{129,385},{257,1},{385... | collective-permute-start | bytes 221192 | tf_op jit(solution)/shard_map/ppermute | solution.py:26
  81.2 4.8 %collective-permute-start.6 = (bf16[144,256]{1,0:T(8,128)(2,1)S(1)}, bf16[144,256]{1,0:T(8,128)(2,1)S(1)}, u32[]{:S(2)}, u32[]{:S(2)}) collective-permute-start(bf16[144,256]{1,0:T(8,128)(2,1)S(1)} %get-tuple-element.12), channel_id=1, source_target_pairs={{0,384},{128,256},{256,128},{384,0},{1,385},{129,257},{257,129},{3... | collective-permute-start | bytes 221192 | tf_op jit(solution)/shard_map/ppermute | solution.py:26
  86.0 1.9 %collective-permute-start.5 = (bf16[144,256]{1,0:T(8,128)(2,1)S(1)}, bf16[144,256]{1,0:T(8,128)(2,1)S(1)}, u32[]{:S(2)}, u32[]{:S(2)}) collective-permute-start(bf16[144,256]{1,0:T(8,128)(2,1)S(1)} %get-tuple-element.11), channel_id=1, source_target_pairs={{0,128},{128,0},{256,384},{384,256},{1,129},{129,1},{257,385},{385... | collective-permute-start | bytes 221192 | tf_op jit(solution)/shard_map/ppermute | solution.py:26
  87.9 0.7 collective-permute-start.12
  88.6 0.0 copy-start.1
  88.6 0.0 collective-permute-done.7.r2
  88.6 4.8 %collective-permute-done.6.r3 = bf16[144,256]{1,0:T(8,128)(2,1)S(1)} collective-permute-done((bf16[144,256]{1,0:T(8,128)(2,1)S(1)}, bf16[144,256]{1,0:T(8,128)(2,1)S(1)}, u32[]{:S(2)}, u32[]{:S(2)}) %collective-permute-start.6) | collective-permute-done | bytes 73760 | tf_op jit(solution)/shard_map/ppermute | solution.py:26
  93.4 19.9 %collective-permute-done.5.r1 = bf16[144,256]{1,0:T(8,128)(2,1)S(1)} collective-permute-done((bf16[144,256]{1,0:T(8,128)(2,1)S(1)}, bf16[144,256]{1,0:T(8,128)(2,1)S(1)}, u32[]{:S(2)}, u32[]{:S(2)}) %collective-permute-start.5) | collective-permute-done | bytes 73760 | tf_op jit(solution)/shard_map/ppermute | solution.py:26
  113.3 0.0 copy-done.1
  113.3 0.1 shard_map.60
  113.4 1.9 %collective-permute-start.10 = (bf16[64,256]{1,0:T(8,128)(2,1)S(1)}, bf16[64,256]{1,0:T(8,128)(2,1)S(1)}, u32[]{:S(2)}, u32[]{:S(2)}) collective-permute-start(bf16[64,256]{1,0:T(8,128)(2,1)S(1)} %shard_map.60), channel_id=1, source_target_pairs={{0,128},{128,0},{256,384},{384,256},{1,129},{129,1},{257,385},{385... | collective-permute-start | bytes 98312 | tf_op jit(solution)/shard_map/ppermute | solution.py:26
  115.3 7.8 %collective-permute-done.10 = bf16[64,256]{1,0:T(8,128)(2,1)S(1)} collective-permute-done((bf16[64,256]{1,0:T(8,128)(2,1)S(1)}, bf16[64,256]{1,0:T(8,128)(2,1)S(1)}, u32[]{:S(2)}, u32[]{:S(2)}) %collective-permute-start.10) | collective-permute-done | bytes 32800 | tf_op jit(solution)/shard_map/ppermute | solution.py:26
  123.1 1.9 %collective-permute-start.11 = (bf16[128,256]{1,0:T(8,128)(2,1)S(1)}, bf16[128,256]{1,0:T(8,128)(2,1)S(1)}, u32[]{:S(2)}, u32[]{:S(2)}) collective-permute-start(bf16[128,256]{1,0:T(8,128)(2,1)S(1)} %pad_maximum_fusion.3), channel_id=1, source_target_pairs={{0,384},{128,256},{256,128},{384,0},{1,385},{129,257},{257,129},{3... | collective-permute-start | bytes 196616 | tf_op jit(solution)/shard_map/ppermute | solution.py:26
  125.0 0.0 collective-permute-done.12
  125.0 8.1 %collective-permute-done.11 = bf16[128,256]{1,0:T(8,128)(2,1)S(1)} collective-permute-done((bf16[128,256]{1,0:T(8,128)(2,1)S(1)}, bf16[128,256]{1,0:T(8,128)(2,1)S(1)}, u32[]{:S(2)}, u32[]{:S(2)}) %collective-permute-start.11) | collective-permute-done | bytes 65568 | tf_op jit(solution)/shard_map/ppermute | solution.py:26
  133.2 1.1 broadcast_in_dim.11
  134.2 3.5 %all-to-all-start.2 = ((bf16[4,256,512]{2,1,0:T(8,128)(2,1)}), bf16[4,256,512]{2,1,0:T(8,128)(2,1)S(1)}, u32[]{:S(2)}, u32[]{:S(2)}) async-start(bf16[4,256,512]{2,1,0:T(8,128)(2,1)} %broadcast_in_dim.11), calls=%async_computation.2 | async-start | bytes 2097152 | tf_op jit(solution)/shard_map/all_to_all | solution.py:228
  137.8 3.9 %collective-permute-start.8 = (bf16[256,256]{1,0:T(8,128)(2,1)S(1)}, bf16[256,256]{1,0:T(8,128)(2,1)S(1)}, u32[]{:S(2)}, u32[]{:S(2)}) collective-permute-start(bf16[256,256]{1,0:T(8,128)(2,1)S(1)} %pad_maximum_fusion.1), channel_id=1, source_target_pairs={{0,32},{32,0},{64,96},{96,64},{1,33},{33,1},{65,97},{97,65},{2,34}... | collective-permute-start | bytes 393224 | tf_op jit(solution)/shard_map/ppermute | solution.py:26
  141.7 9.9 %collective-permute-done.8 = bf16[256,256]{1,0:T(8,128)(2,1)S(1)} collective-permute-done((bf16[256,256]{1,0:T(8,128)(2,1)S(1)}, bf16[256,256]{1,0:T(8,128)(2,1)S(1)}, u32[]{:S(2)}, u32[]{:S(2)}) %collective-permute-start.8) | collective-permute-done | bytes 131104 | tf_op jit(solution)/shard_map/ppermute | solution.py:26
  151.6 3.9 %collective-permute-start.9 = (bf16[512,256]{1,0:T(8,128)(2,1)S(1)}, bf16[512,256]{1,0:T(8,128)(2,1)S(1)}, u32[]{:S(2)}, u32[]{:S(2)}) collective-permute-start(bf16[512,256]{1,0:T(8,128)(2,1)S(1)} %constant_dynamic-update-slice_fusion.1.b0.near), channel_id=1, source_target_pairs={{0,96},{32,64},{64,32},{96,0},{1,97},{33,65},{65,33},{97,1},{2,98}... | collective-permute-start | bytes 786440 | tf_op jit(solution)/shard_map/ppermute | solution.py:26
  155.5 5.5 %collective-permute-done.9.b1.far = bf16[512,256]{1,0:T(8,128)(2,1)S(1)} collective-permute-done((bf16[512,256]{1,0:T(8,128)(2,1)S(1)}, bf16[512,256]{1,0:T(8,128)(2,1)S(1)}, u32[]{:S(2)}, u32[]{:S(2)}) %collective-permute-start.9) | collective-permute-done | bytes 262176 | tf_op jit(solution)/shard_map/ppermute | solution.py:26
  161.1 8.3 %shard_map.61.inverse = f32[256,256]{1,0:T(8,128)S(1)} custom-call(bf16[512,256]{1,0:T(8,128)(2,1)S(1)} %constant_dynamic-update-slice_fusion.1.b0.near, bf16[512,256]{1,0:T(8,128)(2,1)S(1)} %collective-permute-done.9.b1.far), custom_call_target="tpu_custom_call" | custom-call | tf_op jit(solution)/shard_map/pallas_call | solution.py:64
  169.4 0.0 all-to-all-done.2.both
  169.4 1.9 %shard_map.62 = (f32[256,256]{1,0:T(8,128)}, f32[256,256]{1,0:T(8,128)}) custom-call(s32[1]{0:T(128)} %bitcast.1.is_band, bf16[512,256]{1,0:T(8,128)(2,1)S(1)} %constant_dynamic-update-slice_fusion.1.b0.near, bf16[512,256]{1,0:T(8,128)(2,1)S(1)} %collective-permute-done.9.b1.far, bf16[4,256,512]{2,1,0:T(8,128)(2,1)S(1)} %all-to-all-done.2.both, ...), custom_call_target="tpu_custom_call" | custom-call | tf_op jit(solution)/shard_map/pallas_call | solution.py:64
  (23 shorter events, 0.3 us)
Async XLA Ops:
  0.6 2.9 %collective-permute-start = (bf16[64,256]{1,0:T(8,128)(2,1)}, bf16[64,256]{1,0:T(8,128)(2,1)S(1)}, u32[]{:S(2)}, u32[]{:S(2)}) collective-permute-start(bf16[64,256]{1,0:T(8,128)(2,1)} %tokens.1), channel_id=1, source_target_pairs={{0,0},{1,1},{2,2},{3,3},{4,4},{5,5},{6,6},{7,7},{8,128},{9,129},{1... | collective-permute-start | bytes 98312 | tf_op jit(solution)/shard_map/ppermute | solution.py:34
  2.7 0.8 copy-start.2
  42.9 2.1 %copy-start = (bf16[512,256]{1,0:T(8,128)(2,1)S(1)}, bf16[512,256]{1,0:T(8,128)(2,1)}, u32[]{:S(2)}) copy-start(bf16[512,256]{1,0:T(8,128)(2,1)} %p0.1) | copy-start | bytes 786436
  42.9 26.4 %collective-permute-start.1 = (bf16[1088,256]{1,0:T(8,128)(2,1)S(1)}, bf16[1088,256]{1,0:T(8,128)(2,1)S(1)}, u32[]{:S(2)}, u32[]{:S(2)}) collective-permute-start(bf16[1088,256]{1,0:T(8,128)(2,1)S(1)} %fusion.mine), channel_id=1, source_target_pairs={{0,1},{1,0},{2,3},{3,2},{4,5},{5,4},{6,7},{7,6},{8,9},{9,8},{10,11... | collective-permute-start | bytes 1671176 | tf_op jit(solution)/shard_map/ppermute | solution.py:26
  45.0 11.1 %collective-permute-start.2 = (bf16[512,256]{1,0:T(8,128)(2,1)S(1)}, bf16[512,256]{1,0:T(8,128)(2,1)S(1)}, u32[]{:S(2)}, u32[]{:S(2)}) collective-permute-start(bf16[512,256]{1,0:T(8,128)(2,1)S(1)} %copy-done), channel_id=1, source_target_pairs={{0,32},{32,0},{64,96},{96,64},{1,33},{33,1},{65,97},{97,65},{2,34}... | collective-permute-start | bytes 786440 | tf_op jit(solution)/shard_map/ppermute | solution.py:26
  48.5 15.3 %collective-permute-start.3 = (bf16[512,256]{1,0:T(8,128)(2,1)S(1)}, bf16[512,256]{1,0:T(8,128)(2,1)S(1)}, u32[]{:S(2)}, u32[]{:S(2)}) collective-permute-start(bf16[512,256]{1,0:T(8,128)(2,1)S(1)} %copy-done), channel_id=1, source_target_pairs={{0,64},{32,96},{64,0},{96,32},{1,65},{33,97},{65,1},{97,33},{2,66}... | collective-permute-start | bytes 786440 | tf_op jit(solution)/shard_map/ppermute | solution.py:26
  53.3 16.0 %collective-permute-start.4 = (bf16[512,256]{1,0:T(8,128)(2,1)S(1)}, bf16[512,256]{1,0:T(8,128)(2,1)S(1)}, u32[]{:S(2)}, u32[]{:S(2)}) collective-permute-start(bf16[512,256]{1,0:T(8,128)(2,1)S(1)} %copy-done), channel_id=1, source_target_pairs={{0,96},{32,64},{64,32},{96,0},{1,97},{33,65},{65,33},{97,1},{2,98}... | collective-permute-start | bytes 786440 | tf_op jit(solution)/shard_map/ppermute | solution.py:26
  69.9 18.8 %collective-permute-start.7 = (bf16[144,256]{1,0:T(8,128)(2,1)S(1)}, bf16[144,256]{1,0:T(8,128)(2,1)S(1)}, u32[]{:S(2)}, u32[]{:S(2)}) collective-permute-start(bf16[144,256]{1,0:T(8,128)(2,1)S(1)} %get-tuple-element.13), channel_id=1, source_target_pairs={{0,256},{128,384},{256,0},{384,128},{1,257},{129,385},{257,1},{385... | collective-permute-start | bytes 221192 | tf_op jit(solution)/shard_map/ppermute | solution.py:26
  81.2 12.2 %collective-permute-start.6 = (bf16[144,256]{1,0:T(8,128)(2,1)S(1)}, bf16[144,256]{1,0:T(8,128)(2,1)S(1)}, u32[]{:S(2)}, u32[]{:S(2)}) collective-permute-start(bf16[144,256]{1,0:T(8,128)(2,1)S(1)} %get-tuple-element.12), channel_id=1, source_target_pairs={{0,384},{128,256},{256,128},{384,0},{1,385},{129,257},{257,129},{3... | collective-permute-start | bytes 221192 | tf_op jit(solution)/shard_map/ppermute | solution.py:26
  86.0 27.3 %collective-permute-start.5 = (bf16[144,256]{1,0:T(8,128)(2,1)S(1)}, bf16[144,256]{1,0:T(8,128)(2,1)S(1)}, u32[]{:S(2)}, u32[]{:S(2)}) collective-permute-start(bf16[144,256]{1,0:T(8,128)(2,1)S(1)} %get-tuple-element.11), channel_id=1, source_target_pairs={{0,128},{128,0},{256,384},{384,256},{1,129},{129,1},{257,385},{385... | collective-permute-start | bytes 221192 | tf_op jit(solution)/shard_map/ppermute | solution.py:26
  87.9 37.1 %collective-permute-start.12 = (bf16[256,256]{1,0:T(8,128)(2,1)S(1)}, bf16[256,256]{1,0:T(8,128)(2,1)S(1)}, u32[]{:S(2)}, u32[]{:S(2)}) collective-permute-start(bf16[256,256]{1,0:T(8,128)(2,1)S(1)} %get-tuple-element.15), channel_id=1, source_target_pairs={{0,0},{1,1},{2,2},{3,3},{4,4},{5,5},{6,6},{7,7},{8,128},{9,129},{1... | collective-permute-start | bytes 393224 | tf_op jit(solution)/shard_map/ppermute | solution.py:34
  88.6 24.7 %copy-start.1 = (bf16[64,256]{1,0:T(8,128)(2,1)S(1)}, bf16[64,256]{1,0:T(8,128)(2,1)}, u32[]{:S(2)}) copy-start(bf16[64,256]{1,0:T(8,128)(2,1)} %tokens.1) | copy-start | bytes 98308
  113.4 9.7 %collective-permute-start.10 = (bf16[64,256]{1,0:T(8,128)(2,1)S(1)}, bf16[64,256]{1,0:T(8,128)(2,1)S(1)}, u32[]{:S(2)}, u32[]{:S(2)}) collective-permute-start(bf16[64,256]{1,0:T(8,128)(2,1)S(1)} %shard_map.60), channel_id=1, source_target_pairs={{0,128},{128,0},{256,384},{384,256},{1,129},{129,1},{257,385},{385... | collective-permute-start | bytes 98312 | tf_op jit(solution)/shard_map/ppermute | solution.py:26
  123.1 10.1 %collective-permute-start.11 = (bf16[128,256]{1,0:T(8,128)(2,1)S(1)}, bf16[128,256]{1,0:T(8,128)(2,1)S(1)}, u32[]{:S(2)}, u32[]{:S(2)}) collective-permute-start(bf16[128,256]{1,0:T(8,128)(2,1)S(1)} %pad_maximum_fusion.3), channel_id=1, source_target_pairs={{0,384},{128,256},{256,128},{384,0},{1,385},{129,257},{257,129},{3... | collective-permute-start | bytes 196616 | tf_op jit(solution)/shard_map/ppermute | solution.py:26
  134.2 35.2 %all-to-all-start.2 = ((bf16[4,256,512]{2,1,0:T(8,128)(2,1)}), bf16[4,256,512]{2,1,0:T(8,128)(2,1)S(1)}, u32[]{:S(2)}, u32[]{:S(2)}) async-start(bf16[4,256,512]{2,1,0:T(8,128)(2,1)} %broadcast_in_dim.11), calls=%async_computation.2 | async-start | bytes 2097152 | tf_op jit(solution)/shard_map/all_to_all | solution.py:228
  137.8 13.8 %collective-permute-start.8 = (bf16[256,256]{1,0:T(8,128)(2,1)S(1)}, bf16[256,256]{1,0:T(8,128)(2,1)S(1)}, u32[]{:S(2)}, u32[]{:S(2)}) collective-permute-start(bf16[256,256]{1,0:T(8,128)(2,1)S(1)} %pad_maximum_fusion.1), channel_id=1, source_target_pairs={{0,32},{32,0},{64,96},{96,64},{1,33},{33,1},{65,97},{97,65},{2,34}... | collective-permute-start | bytes 393224 | tf_op jit(solution)/shard_map/ppermute | solution.py:26
  151.6 9.5 %collective-permute-start.9 = (bf16[512,256]{1,0:T(8,128)(2,1)S(1)}, bf16[512,256]{1,0:T(8,128)(2,1)S(1)}, u32[]{:S(2)}, u32[]{:S(2)}) collective-permute-start(bf16[512,256]{1,0:T(8,128)(2,1)S(1)} %constant_dynamic-update-slice_fusion.1.b0.near), channel_id=1, source_target_pairs={{0,96},{32,64},{64,32},{96,0},{1,97},{33,65},{65,33},{97,1},{2,98}... | collective-permute-start | bytes 786440 | tf_op jit(solution)/shard_map/ppermute | solution.py:26

commit v4 on v3

--- a/solution.py
+++ b/solution.py
@@ -74,11 +74,8 @@
     return lax.dot_general(a, b, (((0,), (0,)), ((), ())), preferred_element_type=F32)
 
 
-def project_kernel(mine, other, gain, p0, p1, p2, p3, keep, s1, s2, s3, column, acc, sq):
-    zh, y, x, zl, c = [lax.axis_index(a) for a in AXES]
-    for i, z_rel in enumerate((0, 1, 3, 2)):
-        at = pl.multiple_of(64 + ((x ^ z_rel) * 4 + zl) * 64, 64)
-        column[64 * i : 64 * i + 64, :] = mine[pl.ds(at, 64), :]
+def project_kernel(mine, other, gain, own, p0, p1, p2, p3, keep, s1, s2, s3, acc, sq):
+    zh, y, c = [lax.axis_index(a) for a in ("zh", "y", "c")]
     total = jnp.zeros((256, 256), F32)
     squares = jnp.zeros((256, 256), F32)
     for y_rel, proj in enumerate((p0, p1, p2, p3)):
@@ -110,6 +107,7 @@
         out[64:80, :] = jnp.broadcast_to(line, (16, 256)).astype(out.dtype)
         if step:
             out[80:144, :] = mine[0:64, :] + other[0:64, :]
+            out[144:208, :] = own[...]
 
 
 def change_kernel(tokens, keep, r1, r2, r3, change):
@@ -203,19 +201,19 @@
     other = swap(load, "c", 1, 2)
     band = band + other[:64]
 
-    part = jax.ShapeDtypeStruct((144, 256), BF16)
-    block = jax.ShapeDtypeStruct((256, 256), BF16)
-    keep, s1, s2, s3, column = call(
+    part = jax.ShapeDtypeStruct((208, 256), BF16)
+    keep, s1, s2, s3 = call(
         project_kernel,
-        (jax.ShapeDtypeStruct((80, 256), F32), part, part, part, block),
+        (jax.ShapeDtypeStruct((80, 256), F32), part, part, part),
         load,
         other,
         gains,
+        tokens,
         *weights,
         scratch=(pltpu.VMEM((256, 256), F32), pltpu.VMEM((256, 256), F32)),
     )
     r2, r1, r3 = swap(s2, "zh", 2), swap(s1, "zh", 1), swap(s3, "zh", 3)
-    column = transpose(column)
+    column = jnp.concatenate([tokens] + [r[144:208] for r in (r1, r3, r2)], axis=0)
     bands = jnp.concatenate([band] + [r[80:144] for r in (r1, r3, r2)], axis=0)
     bands = double(bands, "y", 1)
     bands = [bands, swap(bands, "y", 3)]

time: 172 us -> 163 us (0.948)
  the two profiles are of different devices: /device:TPU:32 before, /device:TPU:6 now
where the time goes in v4:
time: 163 us; the launch traced here: 160 us
  starting transfers between devices  64 us (39%)
  waiting for transfers between devices  55.2 us (34%)
  blocking collectives  26.4 us (16%)
  Pallas kernels  10.8 us (7%)
  local copies, waits for them, and re-layouts  2 us (1%)
    ppermute x11, waiting for transfers between devices, swap(): return lax.ppermute(value, axis, [(i, i ^ bits) for i in range(size)])  53.7 us
    ppermute x11, starting transfers between devices, swap(): return lax.ppermute(value, axis, [(i, i ^ bits) for i in range(size)])  47.9 us
    all_to_all x2, blocking collectives, spread(): parts = lax.all_to_all(parts, axis, 0, 0, tiled=True)  26.4 us
    ppermute x1, starting transfers between devices, transpose(): lax.ppermute(value, AXES, [(((a * 4 + b) * 4 + d) * 8 + e, ((d * 4 + b) *...  12.7 us
    pallas_call x4, Pallas kernels, call(): pl.pallas_call(kernel, out_shape=outs, in_specs=[smem] * n_scalars + [vme...  10.8 us
    all_to_all x1, starting transfers between devices, steps(): both = lax.all_to_all(both, 'y', 0, 0, tiled=True)  3.51 us
  transfers between devices with their start and end apart: 13, of which 10 were waited for; matrix products, arithmetic and copies ran while one was open for 0% of the time, Pallas kernels for 5%

profile of v4, /device:TPU:6, one launch (start us, length us, event | category | flops | bytes accessed | tf_op | source)
XLA Modules:
  0.0 160.2 jit_solution(2150178115792753297)
XLA Ops:
  0.6 12.7 %collective-permute-start = (bf16[64,256]{1,0:T(8,128)(2,1)}, bf16[64,256]{1,0:T(8,128)(2,1)S(1)}, u32[]{:S(2)}, u32[]{:S(2)}) collective-permute-start(bf16[64,256]{1,0:T(8,128)(2,1)} %tokens.1), channel_id=1, source_target_pairs={{0,0},{1,1},{2,2},{3,3},{4,4},{5,5},{6,6},{7,7},{8,128},{9,129},{1... | collective-permute-start | bytes 98312 | tf_op jit(solution)/shard_map/ppermute | solution.py:34
  13.9 0.0 copy-start.2
  14.0 0.7 copy-done.2
  14.7 1.5 collective-permute-done
  16.3 11.0 %all_to_all.15 = bf16[4,128,256]{2,1,0:T(8,128)(2,1)S(1)} all-to-all(bf16[4,128,256]{2,1,0:T(8,128)(2,1)S(1)} %broadcast_in_dim.9), channel_id=1, replica_groups=mesh['zh'=4,'y'=4,'x'=4,'zl'=4,'c'=2] {'zl'}, dimensions={0} | all-to-all | bytes 524288 | tf_op jit(solution)/shard_map/all_to_all | solution.py:49
  27.4 15.3 %all_to_all.16 = bf16[4,320,256]{2,1,0:T(8,128)(2,1)S(1)} all-to-all(bf16[4,320,256]{2,1,0:T(8,128)(2,1)S(1)} %broadcast_in_dim.10), channel_id=1, replica_groups=mesh['zh'=4,'y'=4,'x'=4,'zl'=4,'c'=2] {'x'}, dimensions={0} | all-to-all | bytes 1310720 | tf_op jit(solution)/shard_map/all_to_all | solution.py:49
  42.8 0.0 copy-start.1
  42.8 0.0 copy-start
  42.9 2.1 %collective-permute-start.1 = (bf16[1088,256]{1,0:T(8,128)(2,1)S(1)}, bf16[1088,256]{1,0:T(8,128)(2,1)S(1)}, u32[]{:S(2)}, u32[]{:S(2)}) collective-permute-start(bf16[1088,256]{1,0:T(8,128)(2,1)S(1)} %fusion.mine), channel_id=1, source_target_pairs={{0,1},{1,0},{2,3},{3,2},{4,5},{5,4},{6,7},{7,6},{8,9},{9,8},{10,11... | collective-permute-start | bytes 1671176 | tf_op jit(solution)/shard_map/ppermute | solution.py:26
  44.9 0.0 copy-done.1
  44.9 3.5 %collective-permute-start.2 = (bf16[512,256]{1,0:T(8,128)(2,1)S(1)}, bf16[512,256]{1,0:T(8,128)(2,1)S(1)}, u32[]{:S(2)}, u32[]{:S(2)}) collective-permute-start(bf16[512,256]{1,0:T(8,128)(2,1)S(1)} %copy-done.1), channel_id=1, source_target_pairs={{0,32},{32,0},{64,96},{96,64},{1,33},{33,1},{65,97},{97,65},{2,34}... | collective-permute-start | bytes 786440 | tf_op jit(solution)/shard_map/ppermute | solution.py:26
  48.4 4.8 %collective-permute-start.3 = (bf16[512,256]{1,0:T(8,128)(2,1)S(1)}, bf16[512,256]{1,0:T(8,128)(2,1)S(1)}, u32[]{:S(2)}, u32[]{:S(2)}) collective-permute-start(bf16[512,256]{1,0:T(8,128)(2,1)S(1)} %copy-done.1), channel_id=1, source_target_pairs={{0,64},{32,96},{64,0},{96,32},{1,65},{33,97},{65,1},{97,33},{2,66}... | collective-permute-start | bytes 786440 | tf_op jit(solution)/shard_map/ppermute | solution.py:26
  53.2 2.1 %collective-permute-start.4 = (bf16[512,256]{1,0:T(8,128)(2,1)S(1)}, bf16[512,256]{1,0:T(8,128)(2,1)S(1)}, u32[]{:S(2)}, u32[]{:S(2)}) collective-permute-start(bf16[512,256]{1,0:T(8,128)(2,1)S(1)} %copy-done.1), channel_id=1, source_target_pairs={{0,96},{32,64},{64,32},{96,0},{1,97},{33,65},{65,33},{97,1},{2,98}... | collective-permute-start | bytes 786440 | tf_op jit(solution)/shard_map/ppermute | solution.py:26
  55.4 0.6 collective-permute-done.2.p1
  56.0 7.7 %collective-permute-done.3.p2 = bf16[512,256]{1,0:T(8,128)(2,1)S(1)} collective-permute-done((bf16[512,256]{1,0:T(8,128)(2,1)S(1)}, bf16[512,256]{1,0:T(8,128)(2,1)S(1)}, u32[]{:S(2)}, u32[]{:S(2)}) %collective-permute-start.3) | collective-permute-done | bytes 262176 | tf_op jit(solution)/shard_map/ppermute | solution.py:26
  63.7 5.5 %collective-permute-done.4.p3 = bf16[512,256]{1,0:T(8,128)(2,1)S(1)} collective-permute-done((bf16[512,256]{1,0:T(8,128)(2,1)S(1)}, bf16[512,256]{1,0:T(8,128)(2,1)S(1)}, u32[]{:S(2)}, u32[]{:S(2)}) %collective-permute-start.4) | collective-permute-done | bytes 262176 | tf_op jit(solution)/shard_map/ppermute | solution.py:26
  69.2 0.0 collective-permute-done.1.other
  69.2 0.0 copy-done
  69.2 0.6 shard_map.59
  69.8 11.3 %collective-permute-start.7 = (bf16[208,256]{1,0:T(8,128)(2,1)S(1)}, bf16[208,256]{1,0:T(8,128)(2,1)S(1)}, u32[]{:S(2)}, u32[]{:S(2)}) collective-permute-start(bf16[208,256]{1,0:T(8,128)(2,1)S(1)} %get-tuple-element.12), channel_id=1, source_target_pairs={{0,256},{128,384},{256,0},{384,128},{1,257},{129,385},{257,1},{385... | collective-permute-start | bytes 319496 | tf_op jit(solution)/shard_map/ppermute | solution.py:26
  81.1 4.8 %collective-permute-start.6 = (bf16[208,256]{1,0:T(8,128)(2,1)S(1)}, bf16[208,256]{1,0:T(8,128)(2,1)S(1)}, u32[]{:S(2)}, u32[]{:S(2)}) collective-permute-start(bf16[208,256]{1,0:T(8,128)(2,1)S(1)} %get-tuple-element.11), channel_id=1, source_target_pairs={{0,384},{128,256},{256,128},{384,0},{1,385},{129,257},{257,129},{3... | collective-permute-start | bytes 319496 | tf_op jit(solution)/shard_map/ppermute | solution.py:26
  85.9 1.9 %collective-permute-start.5 = (bf16[208,256]{1,0:T(8,128)(2,1)S(1)}, bf16[208,256]{1,0:T(8,128)(2,1)S(1)}, u32[]{:S(2)}, u32[]{:S(2)}) collective-permute-start(bf16[208,256]{1,0:T(8,128)(2,1)S(1)} %get-tuple-element.10), channel_id=1, source_target_pairs={{0,128},{128,0},{256,384},{384,256},{1,129},{129,1},{257,385},{385... | collective-permute-start | bytes 319496 | tf_op jit(solution)/shard_map/ppermute | solution.py:26
  87.9 0.0 collective-permute-done.7.r2
  87.9 12.0 %collective-permute-done.6.r3 = bf16[208,256]{1,0:T(8,128)(2,1)S(1)} collective-permute-done((bf16[208,256]{1,0:T(8,128)(2,1)S(1)}, bf16[208,256]{1,0:T(8,128)(2,1)S(1)}, u32[]{:S(2)}, u32[]{:S(2)}) %collective-permute-start.6) | collective-permute-done | bytes 106528 | tf_op jit(solution)/shard_map/ppermute | solution.py:26
  99.9 1.4 collective-permute-done.5.r1
  101.3 0.1 shard_map.60
  101.4 2.4 %collective-permute-start.10 = (bf16[64,256]{1,0:T(8,128)(2,1)S(1)}, bf16[64,256]{1,0:T(8,128)(2,1)S(1)}, u32[]{:S(2)}, u32[]{:S(2)}) collective-permute-start(bf16[64,256]{1,0:T(8,128)(2,1)S(1)} %shard_map.60), channel_id=1, source_target_pairs={{0,128},{128,0},{256,384},{384,256},{1,129},{129,1},{257,385},{385... | collective-permute-start | bytes 98312 | tf_op jit(solution)/shard_map/ppermute | solution.py:26
  103.9 8.1 %collective-permute-done.10 = bf16[64,256]{1,0:T(8,128)(2,1)S(1)} collective-permute-done((bf16[64,256]{1,0:T(8,128)(2,1)S(1)}, bf16[64,256]{1,0:T(8,128)(2,1)S(1)}, u32[]{:S(2)}, u32[]{:S(2)}) %collective-permute-start.10) | collective-permute-done | bytes 32800 | tf_op jit(solution)/shard_map/ppermute | solution.py:26
  112.0 7.1 %collective-permute-start.11 = (bf16[128,256]{1,0:T(8,128)(2,1)S(1)}, bf16[128,256]{1,0:T(8,128)(2,1)S(1)}, u32[]{:S(2)}, u32[]{:S(2)}) collective-permute-start(bf16[128,256]{1,0:T(8,128)(2,1)S(1)} %pad_maximum_fusion.2), channel_id=1, source_target_pairs={{0,384},{128,256},{256,128},{384,0},{1,385},{129,257},{257,129},{3... | collective-permute-start | bytes 196616 | tf_op jit(solution)/shard_map/ppermute | solution.py:26
  119.2 3.0 %collective-permute-done.11 = bf16[128,256]{1,0:T(8,128)(2,1)S(1)} collective-permute-done((bf16[128,256]{1,0:T(8,128)(2,1)S(1)}, bf16[128,256]{1,0:T(8,128)(2,1)S(1)}, u32[]{:S(2)}, u32[]{:S(2)}) %collective-permute-start.11) | collective-permute-done | bytes 65568 | tf_op jit(solution)/shard_map/ppermute | solution.py:26
  122.2 1.1 broadcast_in_dim.11
  123.3 3.5 %all-to-all-start.2 = ((bf16[4,256,512]{2,1,0:T(8,128)(2,1)}), bf16[4,256,512]{2,1,0:T(8,128)(2,1)S(1)}, u32[]{:S(2)}, u32[]{:S(2)}) async-start(bf16[4,256,512]{2,1,0:T(8,128)(2,1)} %broadcast_in_dim.11), calls=%async_computation.2 | async-start | bytes 2097152 | tf_op jit(solution)/shard_map/all_to_all | solution.py:226
  126.8 3.9 %collective-permute-start.8 = (bf16[256,256]{1,0:T(8,128)(2,1)S(1)}, bf16[256,256]{1,0:T(8,128)(2,1)S(1)}, u32[]{:S(2)}, u32[]{:S(2)}) collective-permute-start(bf16[256,256]{1,0:T(8,128)(2,1)S(1)} %pad_maximum_fusion), channel_id=1, source_target_pairs={{0,32},{32,0},{64,96},{96,64},{1,33},{33,1},{65,97},{97,65},{2,34}... | collective-permute-start | bytes 393224 | tf_op jit(solution)/shard_map/ppermute | solution.py:26
  130.7 9.8 %collective-permute-done.8 = bf16[256,256]{1,0:T(8,128)(2,1)S(1)} collective-permute-done((bf16[256,256]{1,0:T(8,128)(2,1)S(1)}, bf16[256,256]{1,0:T(8,128)(2,1)S(1)}, u32[]{:S(2)}, u32[]{:S(2)}) %collective-permute-start.8) | collective-permute-done | bytes 131104 | tf_op jit(solution)/shard_map/ppermute | solution.py:26
  140.5 3.9 %collective-permute-start.9 = (bf16[512,256]{1,0:T(8,128)(2,1)S(1)}, bf16[512,256]{1,0:T(8,128)(2,1)S(1)}, u32[]{:S(2)}, u32[]{:S(2)}) collective-permute-start(bf16[512,256]{1,0:T(8,128)(2,1)S(1)} %constant_dynamic-update-slice_fusion.1.b0.near), channel_id=1, source_target_pairs={{0,96},{32,64},{64,32},{96,0},{1,97},{33,65},{65,33},{97,1},{2,98}... | collective-permute-start | bytes 786440 | tf_op jit(solution)/shard_map/ppermute | solution.py:26
  144.4 5.5 %collective-permute-done.9.b1.far = bf16[512,256]{1,0:T(8,128)(2,1)S(1)} collective-permute-done((bf16[512,256]{1,0:T(8,128)(2,1)S(1)}, bf16[512,256]{1,0:T(8,128)(2,1)S(1)}, u32[]{:S(2)}, u32[]{:S(2)}) %collective-permute-start.9) | collective-permute-done | bytes 262176 | tf_op jit(solution)/shard_map/ppermute | solution.py:26
  150.0 8.3 %shard_map.61.inverse = f32[256,256]{1,0:T(8,128)S(1)} custom-call(bf16[512,256]{1,0:T(8,128)(2,1)S(1)} %constant_dynamic-update-slice_fusion.1.b0.near, bf16[512,256]{1,0:T(8,128)(2,1)S(1)} %collective-permute-done.9.b1.far), custom_call_target="tpu_custom_call" | custom-call | tf_op jit(solution)/shard_map/pallas_call | solution.py:64
  158.3 0.0 all-to-all-done.2.both
  158.3 1.8 %shard_map.62 = (f32[256,256]{1,0:T(8,128)}, f32[256,256]{1,0:T(8,128)}) custom-call(s32[1]{0:T(128)} %bitcast.1.is_band, bf16[512,256]{1,0:T(8,128)(2,1)S(1)} %constant_dynamic-update-slice_fusion.1.b0.near, bf16[512,256]{1,0:T(8,128)(2,1)S(1)} %collective-permute-done.9.b1.far, bf16[4,256,512]{2,1,0:T(8,128)(2,1)S(1)} %all-to-all-done.2.both, ...), custom_call_target="tpu_custom_call" | custom-call | tf_op jit(solution)/shard_map/pallas_call | solution.py:64
  (23 shorter events, 0.3 us)
Async XLA Ops:
  0.6 15.6 %collective-permute-start = (bf16[64,256]{1,0:T(8,128)(2,1)}, bf16[64,256]{1,0:T(8,128)(2,1)S(1)}, u32[]{:S(2)}, u32[]{:S(2)}) collective-permute-start(bf16[64,256]{1,0:T(8,128)(2,1)} %tokens.1), channel_id=1, source_target_pairs={{0,0},{1,1},{2,2},{3,3},{4,4},{5,5},{6,6},{7,7},{8,128},{9,129},{1... | collective-permute-start | bytes 98312 | tf_op jit(solution)/shard_map/ppermute | solution.py:34
  13.9 0.8 copy-start.2
  42.8 2.1 %copy-start.1 = (bf16[512,256]{1,0:T(8,128)(2,1)S(1)}, bf16[512,256]{1,0:T(8,128)(2,1)}, u32[]{:S(2)}) copy-start(bf16[512,256]{1,0:T(8,128)(2,1)} %p0.1) | copy-start | bytes 786436
  42.8 26.4 %copy-start = (bf16[64,256]{1,0:T(8,128)(2,1)S(1)}, bf16[64,256]{1,0:T(8,128)(2,1)}, u32[]{:S(2)}) copy-start(bf16[64,256]{1,0:T(8,128)(2,1)} %tokens.1) | copy-start | bytes 98308
  42.9 26.4 %collective-permute-start.1 = (bf16[1088,256]{1,0:T(8,128)(2,1)S(1)}, bf16[1088,256]{1,0:T(8,128)(2,1)S(1)}, u32[]{:S(2)}, u32[]{:S(2)}) collective-permute-start(bf16[1088,256]{1,0:T(8,128)(2,1)S(1)} %fusion.mine), channel_id=1, source_target_pairs={{0,1},{1,0},{2,3},{3,2},{4,5},{5,4},{6,7},{7,6},{8,9},{9,8},{10,11... | collective-permute-start | bytes 1671176 | tf_op jit(solution)/shard_map/ppermute | solution.py:26
  44.9 11.1 %collective-permute-start.2 = (bf16[512,256]{1,0:T(8,128)(2,1)S(1)}, bf16[512,256]{1,0:T(8,128)(2,1)S(1)}, u32[]{:S(2)}, u32[]{:S(2)}) collective-permute-start(bf16[512,256]{1,0:T(8,128)(2,1)S(1)} %copy-done.1), channel_id=1, source_target_pairs={{0,32},{32,0},{64,96},{96,64},{1,33},{33,1},{65,97},{97,65},{2,34}... | collective-permute-start | bytes 786440 | tf_op jit(solution)/shard_map/ppermute | solution.py:26
  48.4 15.3 %collective-permute-start.3 = (bf16[512,256]{1,0:T(8,128)(2,1)S(1)}, bf16[512,256]{1,0:T(8,128)(2,1)S(1)}, u32[]{:S(2)}, u32[]{:S(2)}) collective-permute-start(bf16[512,256]{1,0:T(8,128)(2,1)S(1)} %copy-done.1), channel_id=1, source_target_pairs={{0,64},{32,96},{64,0},{96,32},{1,65},{33,97},{65,1},{97,33},{2,66}... | collective-permute-start | bytes 786440 | tf_op jit(solution)/shard_map/ppermute | solution.py:26
  53.2 16.0 %collective-permute-start.4 = (bf16[512,256]{1,0:T(8,128)(2,1)S(1)}, bf16[512,256]{1,0:T(8,128)(2,1)S(1)}, u32[]{:S(2)}, u32[]{:S(2)}) collective-permute-start(bf16[512,256]{1,0:T(8,128)(2,1)S(1)} %copy-done.1), channel_id=1, source_target_pairs={{0,96},{32,64},{64,32},{96,0},{1,97},{33,65},{65,33},{97,1},{2,98}... | collective-permute-start | bytes 786440 | tf_op jit(solution)/shard_map/ppermute | solution.py:26
  69.8 18.1 %collective-permute-start.7 = (bf16[208,256]{1,0:T(8,128)(2,1)S(1)}, bf16[208,256]{1,0:T(8,128)(2,1)S(1)}, u32[]{:S(2)}, u32[]{:S(2)}) collective-permute-start(bf16[208,256]{1,0:T(8,128)(2,1)S(1)} %get-tuple-element.12), channel_id=1, source_target_pairs={{0,256},{128,384},{256,0},{384,128},{1,257},{129,385},{257,1},{385... | collective-permute-start | bytes 319496 | tf_op jit(solution)/shard_map/ppermute | solution.py:26
  81.1 18.8 %collective-permute-start.6 = (bf16[208,256]{1,0:T(8,128)(2,1)S(1)}, bf16[208,256]{1,0:T(8,128)(2,1)S(1)}, u32[]{:S(2)}, u32[]{:S(2)}) collective-permute-start(bf16[208,256]{1,0:T(8,128)(2,1)S(1)} %get-tuple-element.11), channel_id=1, source_target_pairs={{0,384},{128,256},{256,128},{384,0},{1,385},{129,257},{257,129},{3... | collective-permute-start | bytes 319496 | tf_op jit(solution)/shard_map/ppermute | solution.py:26
  85.9 15.4 %collective-permute-start.5 = (bf16[208,256]{1,0:T(8,128)(2,1)S(1)}, bf16[208,256]{1,0:T(8,128)(2,1)S(1)}, u32[]{:S(2)}, u32[]{:S(2)}) collective-permute-start(bf16[208,256]{1,0:T(8,128)(2,1)S(1)} %get-tuple-element.10), channel_id=1, source_target_pairs={{0,128},{128,0},{256,384},{384,256},{1,129},{129,1},{257,385},{385... | collective-permute-start | bytes 319496 | tf_op jit(solution)/shard_map/ppermute | solution.py:26
  101.4 10.6 %collective-permute-start.10 = (bf16[64,256]{1,0:T(8,128)(2,1)S(1)}, bf16[64,256]{1,0:T(8,128)(2,1)S(1)}, u32[]{:S(2)}, u32[]{:S(2)}) collective-permute-start(bf16[64,256]{1,0:T(8,128)(2,1)S(1)} %shard_map.60), channel_id=1, source_target_pairs={{0,128},{128,0},{256,384},{384,256},{1,129},{129,1},{257,385},{385... | collective-permute-start | bytes 98312 | tf_op jit(solution)/shard_map/ppermute | solution.py:26
  112.0 10.2 %collective-permute-start.11 = (bf16[128,256]{1,0:T(8,128)(2,1)S(1)}, bf16[128,256]{1,0:T(8,128)(2,1)S(1)}, u32[]{:S(2)}, u32[]{:S(2)}) collective-permute-start(bf16[128,256]{1,0:T(8,128)(2,1)S(1)} %pad_maximum_fusion.2), channel_id=1, source_target_pairs={{0,384},{128,256},{256,128},{384,0},{1,385},{129,257},{257,129},{3... | collective-permute-start | bytes 196616 | tf_op jit(solution)/shard_map/ppermute | solution.py:26
  123.3 35.0 %all-to-all-start.2 = ((bf16[4,256,512]{2,1,0:T(8,128)(2,1)}), bf16[4,256,512]{2,1,0:T(8,128)(2,1)S(1)}, u32[]{:S(2)}, u32[]{:S(2)}) async-start(bf16[4,256,512]{2,1,0:T(8,128)(2,1)} %broadcast_in_dim.11), calls=%async_computation.2 | async-start | bytes 2097152 | tf_op jit(solution)/shard_map/all_to_all | solution.py:226
  126.8 13.7 %collective-permute-start.8 = (bf16[256,256]{1,0:T(8,128)(2,1)S(1)}, bf16[256,256]{1,0:T(8,128)(2,1)S(1)}, u32[]{:S(2)}, u32[]{:S(2)}) collective-permute-start(bf16[256,256]{1,0:T(8,128)(2,1)S(1)} %pad_maximum_fusion), channel_id=1, source_target_pairs={{0,32},{32,0},{64,96},{96,64},{1,33},{33,1},{65,97},{97,65},{2,34}... | collective-permute-start | bytes 393224 | tf_op jit(solution)/shard_map/ppermute | solution.py:26
  140.5 9.5 %collective-permute-start.9 = (bf16[512,256]{1,0:T(8,128)(2,1)S(1)}, bf16[512,256]{1,0:T(8,128)(2,1)S(1)}, u32[]{:S(2)}, u32[]{:S(2)}) collective-permute-start(bf16[512,256]{1,0:T(8,128)(2,1)S(1)} %constant_dynamic-update-slice_fusion.1.b0.near), channel_id=1, source_target_pairs={{0,96},{32,64},{64,32},{96,0},{1,97},{33,65},{65,33},{97,1},{2,98}... | collective-permute-start | bytes 786440 | tf_op jit(solution)/shard_map/ppermute | solution.py:26

commit v5 on v4

--- a/solution.py
+++ b/solution.py
@@ -107,6 +107,7 @@
         out[64:80, :] = jnp.broadcast_to(line, (16, 256)).astype(out.dtype)
         if step:
             out[80:144, :] = mine[0:64, :] + other[0:64, :]
+        if step in (1, 3):
             out[144:208, :] = own[...]
 
 
@@ -202,9 +203,10 @@
     band = band + other[:64]
 
     part = jax.ShapeDtypeStruct((208, 256), BF16)
+    short = jax.ShapeDtypeStruct((144, 256), BF16)
     keep, s1, s2, s3 = call(
         project_kernel,
-        (jax.ShapeDtypeStruct((80, 256), F32), part, part, part),
+        (jax.ShapeDtypeStruct((80, 256), F32), part, short, part),
         load,
         other,
         gains,
@@ -213,13 +215,14 @@
         scratch=(pltpu.VMEM((256, 256), F32), pltpu.VMEM((256, 256), F32)),
     )
     r2, r1, r3 = swap(s2, "zh", 2), swap(s1, "zh", 1), swap(s3, "zh", 3)
-    column = jnp.concatenate([tokens] + [r[144:208] for r in (r1, r3, r2)], axis=0)
     bands = jnp.concatenate([band] + [r[80:144] for r in (r1, r3, r2)], axis=0)
     bands = double(bands, "y", 1)
     bands = [bands, swap(bands, "y", 3)]
 
     change = call(change_kernel, jax.ShapeDtypeStruct((64, 256), BF16), tokens, keep, r1, r2, r3)
-    change = double(change, "zh", 1)
+    there = swap(jnp.concatenate([change, r3[144:208]], axis=0), "zh", 1)
+    change = jnp.concatenate([change, there[:64]], axis=0)
+    column = jnp.concatenate([tokens, r1[144:208], r3[144:208], there[64:]], axis=0)
     change = double(change, "zh", 3)
     both = jnp.concatenate([change, column], axis=1)
     both = jnp.broadcast_to(both[None], (4, *both.shape))

time: 163 us -> 162 us (level); the launches traced: 160 us -> 161 us
  waiting for transfers between devices: 55.2 us -> 57.1 us
    ppermute x11, waiting for transfers between devices: 53.7 us -> 55.6 us  [swap(): return lax.ppermute(value, axis, [(i, i ^ bits) for i in range(size)])]
  transfers between devices with their start and end apart: 13 -> 13, of which waited for: 10 -> 9; matrix products, arithmetic and copies ran while one was open for 0% -> 0% of each run, Pallas kernels for 5% -> 5%
where the time goes in v5:
time: 162 us; the launch traced here: 161 us
  starting transfers between devices  63.1 us (39%)
  waiting for transfers between devices  57.1 us (35%)
  blocking collectives  26.4 us (16%)
  Pallas kernels  10.8 us (7%)
  local copies, waits for them, and re-layouts  1.99 us (1%)
    ppermute x11, waiting for transfers between devices, swap(): return lax.ppermute(value, axis, [(i, i ^ bits) for i in range(size)])  55.6 us
    ppermute x11, starting transfers between devices, swap(): return lax.ppermute(value, axis, [(i, i ^ bits) for i in range(size)])  46.9 us
    all_to_all x2, blocking collectives, spread(): parts = lax.all_to_all(parts, axis, 0, 0, tiled=True)  26.4 us
    ppermute x1, starting transfers between devices, transpose(): lax.ppermute(value, AXES, [(((a * 4 + b) * 4 + d) * 8 + e, ((d * 4 + b) *...  12.7 us
    pallas_call x4, Pallas kernels, call(): pl.pallas_call(kernel, out_shape=outs, in_specs=[smem] * n_scalars + [vme...  10.8 us
    all_to_all x1, starting transfers between devices, steps(): both = lax.all_to_all(both, 'y', 0, 0, tiled=True)  3.51 us
  transfers between devices with their start and end apart: 13, of which 9 were waited for; matrix products, arithmetic and copies ran while one was open for 0% of the time, Pallas kernels for 5%

profile of v5, /device:TPU:6, one launch (start us, length us, event | category | flops | bytes accessed | tf_op | source)
XLA Modules:
  0.0 161.1 jit_solution(12748129858159130307)
XLA Ops:
  0.6 12.7 %collective-permute-start = (bf16[64,256]{1,0:T(8,128)(2,1)}, bf16[64,256]{1,0:T(8,128)(2,1)S(1)}, u32[]{:S(2)}, u32[]{:S(2)}) collective-permute-start(bf16[64,256]{1,0:T(8,128)(2,1)} %tokens.1), channel_id=1, source_target_pairs={{0,0},{1,1},{2,2},{3,3},{4,4},{5,5},{6,6},{7,7},{8,128},{9,129},{1... | collective-permute-start | bytes 98312 | tf_op jit(solution)/shard_map/ppermute | solution.py:34
  13.9 0.0 copy-start.2
  14.0 0.7 copy-done.2
  14.7 1.5 collective-permute-done
  16.3 11.0 %all_to_all.15 = bf16[4,128,256]{2,1,0:T(8,128)(2,1)S(1)} all-to-all(bf16[4,128,256]{2,1,0:T(8,128)(2,1)S(1)} %broadcast_in_dim.9), channel_id=1, replica_groups=mesh['zh'=4,'y'=4,'x'=4,'zl'=4,'c'=2] {'zl'}, dimensions={0} | all-to-all | bytes 524288 | tf_op jit(solution)/shard_map/all_to_all | solution.py:49
  27.4 15.3 %all_to_all.16 = bf16[4,320,256]{2,1,0:T(8,128)(2,1)S(1)} all-to-all(bf16[4,320,256]{2,1,0:T(8,128)(2,1)S(1)} %broadcast_in_dim.10), channel_id=1, replica_groups=mesh['zh'=4,'y'=4,'x'=4,'zl'=4,'c'=2] {'x'}, dimensions={0} | all-to-all | bytes 1310720 | tf_op jit(solution)/shard_map/all_to_all | solution.py:49
  42.8 0.0 copy-start.1
  42.8 0.0 copy-start
  42.9 2.1 %collective-permute-start.1 = (bf16[1088,256]{1,0:T(8,128)(2,1)S(1)}, bf16[1088,256]{1,0:T(8,128)(2,1)S(1)}, u32[]{:S(2)}, u32[]{:S(2)}) collective-permute-start(bf16[1088,256]{1,0:T(8,128)(2,1)S(1)} %fusion.mine), channel_id=1, source_target_pairs={{0,1},{1,0},{2,3},{3,2},{4,5},{5,4},{6,7},{7,6},{8,9},{9,8},{10,11... | collective-permute-start | bytes 1671176 | tf_op jit(solution)/shard_map/ppermute | solution.py:26
  44.9 0.0 copy-done.1
  44.9 3.5 %collective-permute-start.2 = (bf16[512,256]{1,0:T(8,128)(2,1)S(1)}, bf16[512,256]{1,0:T(8,128)(2,1)S(1)}, u32[]{:S(2)}, u32[]{:S(2)}) collective-permute-start(bf16[512,256]{1,0:T(8,128)(2,1)S(1)} %copy-done.1), channel_id=1, source_target_pairs={{0,32},{32,0},{64,96},{96,64},{1,33},{33,1},{65,97},{97,65},{2,34}... | collective-permute-start | bytes 786440 | tf_op jit(solution)/shard_map/ppermute | solution.py:26
  48.4 4.8 %collective-permute-start.3 = (bf16[512,256]{1,0:T(8,128)(2,1)S(1)}, bf16[512,256]{1,0:T(8,128)(2,1)S(1)}, u32[]{:S(2)}, u32[]{:S(2)}) collective-permute-start(bf16[512,256]{1,0:T(8,128)(2,1)S(1)} %copy-done.1), channel_id=1, source_target_pairs={{0,64},{32,96},{64,0},{96,32},{1,65},{33,97},{65,1},{97,33},{2,66}... | collective-permute-start | bytes 786440 | tf_op jit(solution)/shard_map/ppermute | solution.py:26
  53.2 2.1 %collective-permute-start.4 = (bf16[512,256]{1,0:T(8,128)(2,1)S(1)}, bf16[512,256]{1,0:T(8,128)(2,1)S(1)}, u32[]{:S(2)}, u32[]{:S(2)}) collective-permute-start(bf16[512,256]{1,0:T(8,128)(2,1)S(1)} %copy-done.1), channel_id=1, source_target_pairs={{0,96},{32,64},{64,32},{96,0},{1,97},{33,65},{65,33},{97,1},{2,98}... | collective-permute-start | bytes 786440 | tf_op jit(solution)/shard_map/ppermute | solution.py:26
  55.4 0.6 collective-permute-done.2.p1
  56.0 7.7 %collective-permute-done.3.p2 = bf16[512,256]{1,0:T(8,128)(2,1)S(1)} collective-permute-done((bf16[512,256]{1,0:T(8,128)(2,1)S(1)}, bf16[512,256]{1,0:T(8,128)(2,1)S(1)}, u32[]{:S(2)}, u32[]{:S(2)}) %collective-permute-start.3) | collective-permute-done | bytes 262176 | tf_op jit(solution)/shard_map/ppermute | solution.py:26
  63.7 5.5 %collective-permute-done.4.p3 = bf16[512,256]{1,0:T(8,128)(2,1)S(1)} collective-permute-done((bf16[512,256]{1,0:T(8,128)(2,1)S(1)}, bf16[512,256]{1,0:T(8,128)(2,1)S(1)}, u32[]{:S(2)}, u32[]{:S(2)}) %collective-permute-start.4) | collective-permute-done | bytes 262176 | tf_op jit(solution)/shard_map/ppermute | solution.py:26
  69.2 0.0 collective-permute-done.1.other
  69.2 0.0 copy-done
  69.2 0.5 shard_map.59
  69.8 11.3 %collective-permute-start.7 = (bf16[144,256]{1,0:T(8,128)(2,1)S(1)}, bf16[144,256]{1,0:T(8,128)(2,1)S(1)}, u32[]{:S(2)}, u32[]{:S(2)}) collective-permute-start(bf16[144,256]{1,0:T(8,128)(2,1)S(1)} %get-tuple-element.12), channel_id=1, source_target_pairs={{0,256},{128,384},{256,0},{384,128},{1,257},{129,385},{257,1},{385... | collective-permute-start | bytes 221192 | tf_op jit(solution)/shard_map/ppermute | solution.py:26
  81.1 4.8 %collective-permute-start.6 = (bf16[208,256]{1,0:T(8,128)(2,1)S(1)}, bf16[208,256]{1,0:T(8,128)(2,1)S(1)}, u32[]{:S(2)}, u32[]{:S(2)}) collective-permute-start(bf16[208,256]{1,0:T(8,128)(2,1)S(1)} %get-tuple-element.11), channel_id=1, source_target_pairs={{0,384},{128,256},{256,128},{384,0},{1,385},{129,257},{257,129},{3... | collective-permute-start | bytes 319496 | tf_op jit(solution)/shard_map/ppermute | solution.py:26
  85.9 1.9 %collective-permute-start.5 = (bf16[208,256]{1,0:T(8,128)(2,1)S(1)}, bf16[208,256]{1,0:T(8,128)(2,1)S(1)}, u32[]{:S(2)}, u32[]{:S(2)}) collective-permute-start(bf16[208,256]{1,0:T(8,128)(2,1)S(1)} %get-tuple-element.10), channel_id=1, source_target_pairs={{0,128},{128,0},{256,384},{384,256},{1,129},{129,1},{257,385},{385... | collective-permute-start | bytes 319496 | tf_op jit(solution)/shard_map/ppermute | solution.py:26
  87.8 13.8 %collective-permute-done.5.r1 = bf16[208,256]{1,0:T(8,128)(2,1)S(1)} collective-permute-done((bf16[208,256]{1,0:T(8,128)(2,1)S(1)}, bf16[208,256]{1,0:T(8,128)(2,1)S(1)}, u32[]{:S(2)}, u32[]{:S(2)}) %collective-permute-start.5) | collective-permute-done | bytes 106528 | tf_op jit(solution)/shard_map/ppermute | solution.py:26
  101.7 0.0 collective-permute-done.6.r3
  101.7 0.0 collective-permute-done.7.r2
  101.7 0.1 shard_map.60
  101.8 2.7 %collective-permute-start.10 = (bf16[128,256]{1,0:T(8,128)(2,1)S(1)}, bf16[128,256]{1,0:T(8,128)(2,1)S(1)}, u32[]{:S(2)}, u32[]{:S(2)}) collective-permute-start(bf16[128,256]{1,0:T(8,128)(2,1)S(1)} %pad_maximum_fusion.2), channel_id=1, source_target_pairs={{0,128},{128,0},{256,384},{384,256},{1,129},{129,1},{257,385},{385... | collective-permute-start | bytes 196616 | tf_op jit(solution)/shard_map/ppermute | solution.py:26
  104.5 7.4 %collective-permute-done.10 = bf16[128,256]{1,0:T(8,128)(2,1)S(1)} collective-permute-done((bf16[128,256]{1,0:T(8,128)(2,1)S(1)}, bf16[128,256]{1,0:T(8,128)(2,1)S(1)}, u32[]{:S(2)}, u32[]{:S(2)}) %collective-permute-start.10) | collective-permute-done | bytes 65568 | tf_op jit(solution)/shard_map/ppermute | solution.py:26
  111.9 5.8 %collective-permute-start.11 = (bf16[128,256]{1,0:T(8,128)(2,1)S(1)}, bf16[128,256]{1,0:T(8,128)(2,1)S(1)}, u32[]{:S(2)}, u32[]{:S(2)}) collective-permute-start(bf16[128,256]{1,0:T(8,128)(2,1)S(1)} %pad_maximum_fusion.1), channel_id=1, source_target_pairs={{0,384},{128,256},{256,128},{384,0},{1,385},{129,257},{257,129},{3... | collective-permute-start | bytes 196616 | tf_op jit(solution)/shard_map/ppermute | solution.py:26
  117.8 4.2 %collective-permute-done.11 = bf16[128,256]{1,0:T(8,128)(2,1)S(1)} collective-permute-done((bf16[128,256]{1,0:T(8,128)(2,1)S(1)}, bf16[128,256]{1,0:T(8,128)(2,1)S(1)}, u32[]{:S(2)}, u32[]{:S(2)}) %collective-permute-start.11) | collective-permute-done | bytes 65568 | tf_op jit(solution)/shard_map/ppermute | solution.py:26
  122.0 1.1 broadcast_in_dim.11
  123.1 3.5 %all-to-all-start.2 = ((bf16[4,256,512]{2,1,0:T(8,128)(2,1)}), bf16[4,256,512]{2,1,0:T(8,128)(2,1)S(1)}, u32[]{:S(2)}, u32[]{:S(2)}) async-start(bf16[4,256,512]{2,1,0:T(8,128)(2,1)} %broadcast_in_dim.11), calls=%async_computation.2 | async-start | bytes 2097152 | tf_op jit(solution)/shard_map/all_to_all | solution.py:229
  126.6 3.9 %collective-permute-start.8 = (bf16[256,256]{1,0:T(8,128)(2,1)S(1)}, bf16[256,256]{1,0:T(8,128)(2,1)S(1)}, u32[]{:S(2)}, u32[]{:S(2)}) collective-permute-start(bf16[256,256]{1,0:T(8,128)(2,1)S(1)} %pad_maximum_fusion), channel_id=1, source_target_pairs={{0,32},{32,0},{64,96},{96,64},{1,33},{33,1},{65,97},{97,65},{2,34}... | collective-permute-start | bytes 393224 | tf_op jit(solution)/shard_map/ppermute | solution.py:26
  130.5 10.9 %collective-permute-done.8 = bf16[256,256]{1,0:T(8,128)(2,1)S(1)} collective-permute-done((bf16[256,256]{1,0:T(8,128)(2,1)S(1)}, bf16[256,256]{1,0:T(8,128)(2,1)S(1)}, u32[]{:S(2)}, u32[]{:S(2)}) %collective-permute-start.8) | collective-permute-done | bytes 131104 | tf_op jit(solution)/shard_map/ppermute | solution.py:26
  141.4 4.0 %collective-permute-start.9 = (bf16[512,256]{1,0:T(8,128)(2,1)S(1)}, bf16[512,256]{1,0:T(8,128)(2,1)S(1)}, u32[]{:S(2)}, u32[]{:S(2)}) collective-permute-start(bf16[512,256]{1,0:T(8,128)(2,1)S(1)} %constant_dynamic-update-slice_fusion.1.b0.near), channel_id=1, source_target_pairs={{0,96},{32,64},{64,32},{96,0},{1,97},{33,65},{65,33},{97,1},{2,98}... | collective-permute-start | bytes 786440 | tf_op jit(solution)/shard_map/ppermute | solution.py:26
  145.4 5.5 %collective-permute-done.9.b1.far = bf16[512,256]{1,0:T(8,128)(2,1)S(1)} collective-permute-done((bf16[512,256]{1,0:T(8,128)(2,1)S(1)}, bf16[512,256]{1,0:T(8,128)(2,1)S(1)}, u32[]{:S(2)}, u32[]{:S(2)}) %collective-permute-start.9) | collective-permute-done | bytes 262176 | tf_op jit(solution)/shard_map/ppermute | solution.py:26
  150.9 8.3 %shard_map.61.inverse = f32[256,256]{1,0:T(8,128)S(1)} custom-call(bf16[512,256]{1,0:T(8,128)(2,1)S(1)} %constant_dynamic-update-slice_fusion.1.b0.near, bf16[512,256]{1,0:T(8,128)(2,1)S(1)} %collective-permute-done.9.b1.far), custom_call_target="tpu_custom_call" | custom-call | tf_op jit(solution)/shard_map/pallas_call | solution.py:64
  159.2 0.0 all-to-all-done.2.both
  159.2 1.9 %shard_map.62 = (f32[256,256]{1,0:T(8,128)}, f32[256,256]{1,0:T(8,128)}) custom-call(s32[1]{0:T(128)} %bitcast.1.is_band, bf16[512,256]{1,0:T(8,128)(2,1)S(1)} %constant_dynamic-update-slice_fusion.1.b0.near, bf16[512,256]{1,0:T(8,128)(2,1)S(1)} %collective-permute-done.9.b1.far, bf16[4,256,512]{2,1,0:T(8,128)(2,1)S(1)} %all-to-all-done.2.both, ...), custom_call_target="tpu_custom_call" | custom-call | tf_op jit(solution)/shard_map/pallas_call | solution.py:64
  (25 shorter events, 0.3 us)
Async XLA Ops:
  0.6 15.6 %collective-permute-start = (bf16[64,256]{1,0:T(8,128)(2,1)}, bf16[64,256]{1,0:T(8,128)(2,1)S(1)}, u32[]{:S(2)}, u32[]{:S(2)}) collective-permute-start(bf16[64,256]{1,0:T(8,128)(2,1)} %tokens.1), channel_id=1, source_target_pairs={{0,0},{1,1},{2,2},{3,3},{4,4},{5,5},{6,6},{7,7},{8,128},{9,129},{1... | collective-permute-start | bytes 98312 | tf_op jit(solution)/shard_map/ppermute | solution.py:34
  13.9 0.8 copy-start.2
  42.8 2.1 %copy-start.1 = (bf16[512,256]{1,0:T(8,128)(2,1)S(1)}, bf16[512,256]{1,0:T(8,128)(2,1)}, u32[]{:S(2)}) copy-start(bf16[512,256]{1,0:T(8,128)(2,1)} %p0.1) | copy-start | bytes 786436
  42.8 26.4 %copy-start = (bf16[64,256]{1,0:T(8,128)(2,1)S(1)}, bf16[64,256]{1,0:T(8,128)(2,1)}, u32[]{:S(2)}) copy-start(bf16[64,256]{1,0:T(8,128)(2,1)} %tokens.1) | copy-start | bytes 98308
  42.9 26.4 %collective-permute-start.1 = (bf16[1088,256]{1,0:T(8,128)(2,1)S(1)}, bf16[1088,256]{1,0:T(8,128)(2,1)S(1)}, u32[]{:S(2)}, u32[]{:S(2)}) collective-permute-start(bf16[1088,256]{1,0:T(8,128)(2,1)S(1)} %fusion.mine), channel_id=1, source_target_pairs={{0,1},{1,0},{2,3},{3,2},{4,5},{5,4},{6,7},{7,6},{8,9},{9,8},{10,11... | collective-permute-start | bytes 1671176 | tf_op jit(solution)/shard_map/ppermute | solution.py:26
  44.9 11.1 %collective-permute-start.2 = (bf16[512,256]{1,0:T(8,128)(2,1)S(1)}, bf16[512,256]{1,0:T(8,128)(2,1)S(1)}, u32[]{:S(2)}, u32[]{:S(2)}) collective-permute-start(bf16[512,256]{1,0:T(8,128)(2,1)S(1)} %copy-done.1), channel_id=1, source_target_pairs={{0,32},{32,0},{64,96},{96,64},{1,33},{33,1},{65,97},{97,65},{2,34}... | collective-permute-start | bytes 786440 | tf_op jit(solution)/shard_map/ppermute | solution.py:26
  48.4 15.3 %collective-permute-start.3 = (bf16[512,256]{1,0:T(8,128)(2,1)S(1)}, bf16[512,256]{1,0:T(8,128)(2,1)S(1)}, u32[]{:S(2)}, u32[]{:S(2)}) collective-permute-start(bf16[512,256]{1,0:T(8,128)(2,1)S(1)} %copy-done.1), channel_id=1, source_target_pairs={{0,64},{32,96},{64,0},{96,32},{1,65},{33,97},{65,1},{97,33},{2,66}... | collective-permute-start | bytes 786440 | tf_op jit(solution)/shard_map/ppermute | solution.py:26
  53.2 16.0 %collective-permute-start.4 = (bf16[512,256]{1,0:T(8,128)(2,1)S(1)}, bf16[512,256]{1,0:T(8,128)(2,1)S(1)}, u32[]{:S(2)}, u32[]{:S(2)}) collective-permute-start(bf16[512,256]{1,0:T(8,128)(2,1)S(1)} %copy-done.1), channel_id=1, source_target_pairs={{0,96},{32,64},{64,32},{96,0},{1,97},{33,65},{65,33},{97,1},{2,98}... | collective-permute-start | bytes 786440 | tf_op jit(solution)/shard_map/ppermute | solution.py:26
  69.8 31.9 %collective-permute-start.7 = (bf16[144,256]{1,0:T(8,128)(2,1)S(1)}, bf16[144,256]{1,0:T(8,128)(2,1)S(1)}, u32[]{:S(2)}, u32[]{:S(2)}) collective-permute-start(bf16[144,256]{1,0:T(8,128)(2,1)S(1)} %get-tuple-element.12), channel_id=1, source_target_pairs={{0,256},{128,384},{256,0},{384,128},{1,257},{129,385},{257,1},{385... | collective-permute-start | bytes 221192 | tf_op jit(solution)/shard_map/ppermute | solution.py:26
  81.1 20.6 %collective-permute-start.6 = (bf16[208,256]{1,0:T(8,128)(2,1)S(1)}, bf16[208,256]{1,0:T(8,128)(2,1)S(1)}, u32[]{:S(2)}, u32[]{:S(2)}) collective-permute-start(bf16[208,256]{1,0:T(8,128)(2,1)S(1)} %get-tuple-element.11), channel_id=1, source_target_pairs={{0,384},{128,256},{256,128},{384,0},{1,385},{129,257},{257,129},{3... | collective-permute-start | bytes 319496 | tf_op jit(solution)/shard_map/ppermute | solution.py:26
  85.9 15.8 %collective-permute-start.5 = (bf16[208,256]{1,0:T(8,128)(2,1)S(1)}, bf16[208,256]{1,0:T(8,128)(2,1)S(1)}, u32[]{:S(2)}, u32[]{:S(2)}) collective-permute-start(bf16[208,256]{1,0:T(8,128)(2,1)S(1)} %get-tuple-element.10), channel_id=1, source_target_pairs={{0,128},{128,0},{256,384},{384,256},{1,129},{129,1},{257,385},{385... | collective-permute-start | bytes 319496 | tf_op jit(solution)/shard_map/ppermute | solution.py:26
  101.8 10.1 %collective-permute-start.10 = (bf16[128,256]{1,0:T(8,128)(2,1)S(1)}, bf16[128,256]{1,0:T(8,128)(2,1)S(1)}, u32[]{:S(2)}, u32[]{:S(2)}) collective-permute-start(bf16[128,256]{1,0:T(8,128)(2,1)S(1)} %pad_maximum_fusion.2), channel_id=1, source_target_pairs={{0,128},{128,0},{256,384},{384,256},{1,129},{129,1},{257,385},{385... | collective-permute-start | bytes 196616 | tf_op jit(solution)/shard_map/ppermute | solution.py:26
  111.9 10.1 %collective-permute-start.11 = (bf16[128,256]{1,0:T(8,128)(2,1)S(1)}, bf16[128,256]{1,0:T(8,128)(2,1)S(1)}, u32[]{:S(2)}, u32[]{:S(2)}) collective-permute-start(bf16[128,256]{1,0:T(8,128)(2,1)S(1)} %pad_maximum_fusion.1), channel_id=1, source_target_pairs={{0,384},{128,256},{256,128},{384,0},{1,385},{129,257},{257,129},{3... | collective-permute-start | bytes 196616 | tf_op jit(solution)/shard_map/ppermute | solution.py:26
  123.1 36.1 %all-to-all-start.2 = ((bf16[4,256,512]{2,1,0:T(8,128)(2,1)}), bf16[4,256,512]{2,1,0:T(8,128)(2,1)S(1)}, u32[]{:S(2)}, u32[]{:S(2)}) async-start(bf16[4,256,512]{2,1,0:T(8,128)(2,1)} %broadcast_in_dim.11), calls=%async_computation.2 | async-start | bytes 2097152 | tf_op jit(solution)/shard_map/all_to_all | solution.py:229
  126.6 14.7 %collective-permute-start.8 = (bf16[256,256]{1,0:T(8,128)(2,1)S(1)}, bf16[256,256]{1,0:T(8,128)(2,1)S(1)}, u32[]{:S(2)}, u32[]{:S(2)}) collective-permute-start(bf16[256,256]{1,0:T(8,128)(2,1)S(1)} %pad_maximum_fusion), channel_id=1, source_target_pairs={{0,32},{32,0},{64,96},{96,64},{1,33},{33,1},{65,97},{97,65},{2,34}... | collective-permute-start | bytes 393224 | tf_op jit(solution)/shard_map/ppermute | solution.py:26
  141.4 9.5 %collective-permute-start.9 = (bf16[512,256]{1,0:T(8,128)(2,1)S(1)}, bf16[512,256]{1,0:T(8,128)(2,1)S(1)}, u32[]{:S(2)}, u32[]{:S(2)}) collective-permute-start(bf16[512,256]{1,0:T(8,128)(2,1)S(1)} %constant_dynamic-update-slice_fusion.1.b0.near), channel_id=1, source_target_pairs={{0,96},{32,64},{64,32},{96,0},{1,97},{33,65},{65,33},{97,1},{2,98}... | collective-permute-start | bytes 786440 | tf_op jit(solution)/shard_map/ppermute | solution.py:26
